TPU v7x, 256 devices: a whole 4x4x8 slice. The times are simulated.
256 devices in a mesh: bus: 64 (over y, z_lo, x), harm: 4 (over z_hi, core).
Axes of the slice: x: 4, y: 4, z: 8 (z_hi: 2, z_lo: 4; z = z_hi * 4 + z_lo), core: 2. Of those that a mesh axis runs over, the one named last changes fastest.
Arguments:
- injection: bfloat16 [64, 192, 32, 128], P('harm', 'bus'), may hold values from -6 to 6
- inv_diag: bfloat16 [64, 192, 128, 128], P('harm', 'bus'), may hold values from -0.5 to 0.5
- off_tiles: bfloat16 [64, 192, 3, 128, 128], P('harm', 'bus'), may hold values from -0.15625 to 0.15625
- pattern: int32 [192, 3], P('bus'), may hold values from 0 to 191, as said below
- coupling: bfloat16 [1024, 6, 64, 384], P('bus', None, 'harm'), may hold values from -0.15625 to 0.15625
- site_map: int32 [1024], P('bus'), may hold values from 0 to 63, as said below
- bus_map: int32 [1024], P('bus'), may hold values from 0 to 63
Outputs:
- voltage: float32 [64, 192, 32, 128], P('harm', 'bus')
Inputs may be any that keep to these rules, and one draw needn't show every extreme that they name: `pattern`: each tile row has one column in its own site other than itself, and one in each neighbouring site, a second own one where no neighbour exists. `site_map`: the slot's own index of bus, or one of its two neighbours.
All inputs are finite; a program needn't handle non-finite values.
Results may differ from a plain program's by a relative error of at most 0.0037.
Values may be sent and summed in bfloat16 or wider, within the bound.
A program may use at most 64 MiB of HBM per device.

v0:
```python
import jax
import jax.numpy as jnp
from jax import lax
from jax.sharding import PartitionSpec as P

ITERS = 2


def extended(cells, sides, width):
    for axis, dim in sides:
        count = lax.axis_size(axis)
        ends = count - 1
        head = lax.slice_in_dim(cells, 0, width, axis=dim)
        tail = lax.slice_in_dim(cells, cells.shape[dim] - width, cells.shape[dim], axis=dim)
        cells = jnp.concatenate(
            [
                lax.ppermute(tail, axis, [(i, (i + 1) % count) for i in range(ends)]),
                cells,
                lax.ppermute(head, axis, [((i + 1) % count, i) for i in range(ends)]),
            ],
            axis=dim,
        )
    return cells


def per_device(injection, inv_diag, off_tiles, pattern, coupling, site_map, bus_map):
    harm_dev, tiles_dev, scenarios, tile_width = injection.shape
    half = tile_width // 2
    blocks_dev = tiles_dev // 3
    conv_dev = coupling.shape[0]
    links = pattern.shape[1]
    device = lax.axis_index("bus")
    local_index = pattern - (device - 1) * tiles_dev
    maps = jnp.stack([site_map + 1, bus_map], axis=1)
    near_maps = extended(maps, (("bus", 0),), conv_dev)
    mine = near_maps[:, 0] == device + 1
    targets = jnp.arange(blocks_dev * half, dtype=jnp.int32)
    hits = ((near_maps[:, 1][:, None] == targets[None, :]) & mine[:, None]).astype(jnp.bfloat16)
    own_shard = site_map - device + 1
    bus_block = bus_map // half
    bus_row = bus_map % half
    voltage = jnp.einsum("htsa,htab->htsb", injection, inv_diag, preferred_element_type=jnp.float32)
    first_links = 1
    for sweep in range(ITERS):
        rounded = voltage.astype(jnp.bfloat16)
        own_columns = jnp.take(rounded, pattern[:, 0] - device * tiles_dev, axis=1)
        network = jnp.einsum(
            "htsa,htab->htsb", own_columns, off_tiles[:, :, 0], preferred_element_type=jnp.float32
        )
        window = extended(rounded, (("bus", 1),), tiles_dev)
        rest = links - first_links
        picked = jnp.take(window, local_index[:, first_links:].reshape(-1), axis=1)
        picked = picked.reshape(harm_dev, tiles_dev, rest, scenarios, tile_width)
        network = network + jnp.einsum(
            "htksa,htkab->htsb",
            picked,
            off_tiles[:, :, first_links:],
            preferred_element_type=jnp.float32,
        )
        grid = window.reshape(harm_dev, 3, 3, blocks_dev, scenarios, 2, half).transpose(
            1, 3, 6, 4, 0, 5, 2
        )
        terminal = grid[own_shard, bus_block, bus_row].reshape(conv_dev, scenarios, harm_dev, 6)
        piece = lax.all_gather(terminal, "harm", axis=2, tiled=True)
        count = piece.shape[2]
        flat = piece.reshape(conv_dev, scenarios, count * 6)
        currents = jnp.einsum(
            "csi,cohi->csoh", flat, coupling, preferred_element_type=jnp.float32
        ).astype(jnp.bfloat16)
        near_currents = extended(currents, (("bus", 0),), conv_dev)
        injected = jnp.einsum(
            "cb,csoh->bsoh", hits, near_currents, preferred_element_type=jnp.float32
        )
        injected = injected.reshape(blocks_dev, half, scenarios, 2, 3, harm_dev).transpose(
            5, 4, 0, 2, 3, 1
        )
        injected = injected.reshape(harm_dev, tiles_dev, scenarios, tile_width)
        residual = (injection.astype(jnp.float32) - network - injected).astype(jnp.bfloat16)
        voltage = jnp.einsum(
            "htsa,htab->htsb", residual, inv_diag, preferred_element_type=jnp.float32
        )
    return voltage


def solution(mesh):
    in_specs = (
        P("harm", "bus", None, None),
        P("harm", "bus", None, None),
        P("harm", "bus", None, None, None),
        P("bus", None),
        P("bus", None, "harm", None),
        P("bus"),
        P("bus"),
    )
    out_specs = P("harm", "bus", None, None)
    return jax.shard_map(
        per_device, mesh=mesh, in_specs=in_specs, out_specs=out_specs, check_vma=False
    )
```

profile of v0, /device:TPU:24, one launch (start us, length us, event | category | flops | bytes accessed | tf_op | source)
XLA Modules:
  0.0 192.2 jit_solution(6981747454849418790)
XLA Ops:
  0.0 0.8 add_bitcast_fusion
  0.8 0.7 pad_add_fusion
  1.5 9.0 %collective-permute-start.3 = (s32[16,2]{0,1:T(2,128)S(1)}, s32[16,2]{0,1:T(2,128)S(1)}, u32[]{:S(2)}, u32[]{:S(2)}) collective-permute-start(s32[16,2]{0,1:T(2,128)S(1)} %pad_add_fusion), channel_id=1, source_target_pairs={{4,0},{8,4},{12,8},{16,12},{20,16},{24,20},{28,24},{32,28},{36,32}... | collective-permute-start | bytes 392 | tf_op jit(solution)/shard_map/ppermute | solution.py:19
  10.5 1.9 collective-permute-start.2
  12.5 1.5 convolution_convert_fusion.1
  14.0 8.7 %collective-permute-start.1 = (bf16[16,3,32,128]{3,2,1,0:T(8,128)(2,1)S(1)}, bf16[16,3,32,128]{3,2,1,0:T(8,128)(2,1)S(1)}, u32[]{:S(2)}, u32[]{:S(2)}) collective-permute-start(bf16[16,3,32,128]{3,2,1,0:T(8,128)(2,1)S(1)} %convolution_convert_fusion.1), channel_id=1, source_target_pairs={{4,0},{8,4},{12,8},{16,12},{20,16},{24,20},{28,24},{32,28},{36,32}... | collective-permute-start | bytes 1179656 | tf_op jit(solution)/shard_map/ppermute | solution.py:19
  22.7 1.9 collective-permute-start
  24.7 0.1 subtract_reduce_fusion
  24.8 0.1 slice.24
  24.9 0.1 reshape.52
  25.0 0.6 compare_and_fusion.1
  25.6 1.3 gather_fusion.2
  26.9 0.1 pad_add_fusion.1
  27.0 0.5 slice_bitcast_fusion
  27.5 0.6 compare_bitcast_fusion
  28.1 2.4 %collective-permute-done.1 = bf16[16,3,32,128]{3,2,1,0:T(8,128)(2,1)S(1)} collective-permute-done((bf16[16,3,32,128]{3,2,1,0:T(8,128)(2,1)S(1)}, bf16[16,3,32,128]{3,2,1,0:T(8,128)(2,1)S(1)}, u32[]{:S(2)}, u32[]{:S(2)}) %collective-permute-start.1) | collective-permute-done | bytes 393248 | tf_op jit(solution)/shard_map/ppermute | solution.py:19
  30.5 9.0 %collective-permute-done = bf16[16,3,32,128]{3,2,1,0:T(8,128)(2,1)} collective-permute-done((bf16[16,3,32,128]{3,2,1,0:T(8,128)(2,1)S(1)}, bf16[16,3,32,128]{3,2,1,0:T(8,128)(2,1)}, u32[]{:S(2)}, u32[]{:S(2)}) %collective-permute-start) | collective-permute-done | bytes 393248 | tf_op jit(solution)/shard_map/ppermute | solution.py:17
  39.5 1.1 pad_maximum_fusion
  40.7 2.5 %reshape.54 = bf16[16,3,3,1,32,2,64]{6,5,4,2,1,0,3:T(2,128)(2,1)} reshape(bf16[16,9,32,128]{3,2,1,0:T(8,128)(2,1)S(1)} %pad_maximum_fusion) | data formatting | bytes 2359296 | tf_op jit(solution)/shard_map/reshape | solution.py:60
  43.2 10.6 %copy.12 = bf16[16,3,3,1,32,2,64]{4,0,5,2,6,3,1:T(8,128)(2,1)} copy(bf16[16,3,3,1,32,2,64]{6,5,4,2,1,0,3:T(2,128)(2,1)} %reshape.54) | data formatting | bytes 2359296 | tf_op jit(solution)/shard_map/reshape | solution.py:60
  53.8 3.0 %gather_fusion = bf16[16,32,16,2,3]{1,2,3,4,0:T(8,128)(2,1)S(1)} fusion(bf16[3,1,64,32,16,2,3]{3,4,5,6,2,1,0:T(8,128)(2,1)} %bitcast.92, s32[16]{0:T(128)S(1)} %get-tuple-element.8), kind=kCustom, calls=%fused_computation.4 | custom fusion | bytes 196800 | tf_op jit(solution)/shard_map/gather | solution.py:63
  56.8 19.6 %all_gather.6 = bf16[16,32,64,6]{1,2,3,0:T(8,128)(2,1)S(1)} all-gather(bf16[16,32,16,6]{1,2,3,0:T(8,128)(2,1)S(1)} %bitcast.100), channel_id=1, replica_groups=mesh['bus'=64,'harm'=4] {'harm'}, dimensions={2}, use_global_device_ids=true | all-gather | bytes 491520 | tf_op jit(solution)/shard_map/all_gather | solution.py:64
  76.4 1.0 copy.14
  77.4 0.2 copy-done.11
  77.7 0.8 fusion.44
  78.4 2.4 %collective-permute-start.5 = (bf16[16,32,6,16]{1,3,2,0:T(8,128)(2,1)S(1)}, bf16[16,32,6,16]{1,3,2,0:T(8,128)(2,1)S(1)}, u32[]{:S(2)}, u32[]{:S(2)}) collective-permute-start(bf16[16,32,6,16]{1,3,2,0:T(8,128)(2,1)S(1)} %fusion.44), channel_id=1, source_target_pairs={{4,0},{8,4},{12,8},{16,12},{20,16},{24,20},{28,24},{32,28},{36,32}... | collective-permute-start | bytes 294920 | tf_op jit(solution)/shard_map/ppermute | solution.py:19
  80.9 3.4 %collective-permute-start.4 = (bf16[16,32,6,16]{1,3,2,0:T(8,128)(2,1)S(1)}, bf16[16,32,6,16]{1,3,2,0:T(8,128)(2,1)}, u32[]{:S(2)}, u32[]{:S(2)}) collective-permute-start(bf16[16,32,6,16]{1,3,2,0:T(8,128)(2,1)S(1)} %fusion.44), channel_id=1, source_target_pairs={{0,4},{4,8},{8,12},{12,16},{16,20},{20,24},{24,28},{28,32},{32,36}... | collective-permute-start | bytes 294920 | tf_op jit(solution)/shard_map/ppermute | solution.py:17
  84.3 1.6 gather_fusion.3
  85.8 1.3 broadcast_select_fusion.1
  87.1 3.3 %fusion.32 = f32[16,3,32,128]{3,2,1,0:T(8,128)} fusion(bf16[16,3,3,128,128]{4,3,2,1,0:T(8,128)(2,1)} %param.13, bf16[16,3,2,32,128]{4,3,0,2,1:T(8,128)(2,1)S(1)} %bitcast.97), kind=kOutput, calls=%fused_computation.26 | convolution fusion | flops 100663296 | bytes 4718592 | tf_op jit(solution)/shard_map/htksa,htkab->htsb/dot_general | solution.py:54
  90.5 1.2 collective-permute-done.5
  91.7 7.1 %collective-permute-done.4 = bf16[16,32,6,16]{1,3,2,0:T(8,128)(2,1)} collective-permute-done((bf16[16,32,6,16]{1,3,2,0:T(8,128)(2,1)S(1)}, bf16[16,32,6,16]{1,3,2,0:T(8,128)(2,1)}, u32[]{:S(2)}, u32[]{:S(2)}) %collective-permute-start.4) | collective-permute-done | bytes 98336 | tf_op jit(solution)/shard_map/ppermute | solution.py:17
  98.8 1.3 pad_maximum_fusion.1
  100.0 0.6 fusion.57
  100.6 1.4 copy.17
  102.0 1.8 reshape.58
  103.8 2.9 %convolution_convert_fusion = bf16[16,3,32,128]{3,2,1,0:T(8,128)(2,1)S(1)} fusion(bf16[16,3,128,128]{3,2,1,0:T(8,128)(2,1)S(1)} %copy-done, f32[16,3,32,128]{3,2,1,0:T(8,128)} %reshape.58, f32[16,3,32,128]{3,2,1,0:T(8,128)} %fusion.32, bf16[16,3,3,128,128]{4,3,2,1,0:T(8,128)(2,1)} %param.13, bf16[16,3,32,128]{3,2,1,0:T(8,128)(2,1)S(1)} %copy-done.1, ...), kind=kOutput, calls=%fused_computation.30 | convolution fusion | flops 102039552 | bytes 5898243 | tf_op jit(solution)/shard_map/htsa,htab->htsb/dot_general | solution.py:79
  106.7 1.9 collective-permute-start.7
  108.7 3.9 %collective-permute-start.6 = (bf16[16,3,32,128]{3,2,1,0:T(8,128)(2,1)S(1)}, bf16[16,3,32,128]{3,2,1,0:T(8,128)(2,1)}, u32[]{:S(2)}, u32[]{:S(2)}) collective-permute-start(bf16[16,3,32,128]{3,2,1,0:T(8,128)(2,1)S(1)} %convolution_convert_fusion), channel_id=1, source_target_pairs={{0,4},{4,8},{8,12},{12,16},{16,20},{20,24},{24,28},{28,32},{32,36}... | collective-permute-start | bytes 1179656 | tf_op jit(solution)/shard_map/ppermute | solution.py:17
  112.6 1.3 gather_fusion.4
  113.9 4.9 %collective-permute-done.7 = bf16[16,3,32,128]{3,2,1,0:T(8,128)(2,1)S(1)} collective-permute-done((bf16[16,3,32,128]{3,2,1,0:T(8,128)(2,1)S(1)}, bf16[16,3,32,128]{3,2,1,0:T(8,128)(2,1)S(1)}, u32[]{:S(2)}, u32[]{:S(2)}) %collective-permute-start.7) | collective-permute-done | bytes 393248 | tf_op jit(solution)/shard_map/ppermute | solution.py:19
  118.9 0.7 copy-done.3
  119.6 6.1 %collective-permute-done.6 = bf16[16,3,32,128]{3,2,1,0:T(8,128)(2,1)} collective-permute-done((bf16[16,3,32,128]{3,2,1,0:T(8,128)(2,1)S(1)}, bf16[16,3,32,128]{3,2,1,0:T(8,128)(2,1)}, u32[]{:S(2)}, u32[]{:S(2)}) %collective-permute-start.6) | collective-permute-done | bytes 393248 | tf_op jit(solution)/shard_map/ppermute | solution.py:17
  125.7 1.2 pad_maximum_fusion.2
  126.9 1.6 gather_fusion.5
  128.5 2.5 %reshape.60 = bf16[16,3,3,1,32,2,64]{6,5,4,2,1,0,3:T(2,128)(2,1)} reshape(bf16[16,9,32,128]{3,2,1,0:T(8,128)(2,1)S(1)} %pad_maximum_fusion.2) | data formatting | bytes 2359296 | tf_op jit(solution)/shard_map/reshape | solution.py:60
  131.0 10.6 %copy.18 = bf16[16,3,3,1,32,2,64]{4,0,5,2,6,3,1:T(8,128)(2,1)} copy(bf16[16,3,3,1,32,2,64]{6,5,4,2,1,0,3:T(2,128)(2,1)} %reshape.60) | data formatting | bytes 2359296 | tf_op jit(solution)/shard_map/reshape | solution.py:60
  141.6 3.0 %gather_fusion.1 = bf16[16,32,16,2,3]{1,2,3,4,0:T(8,128)(2,1)S(1)} fusion(bf16[3,1,64,32,16,2,3]{3,4,5,6,2,1,0:T(8,128)(2,1)} %bitcast.93, s32[16]{0:T(128)S(1)} %get-tuple-element.8), kind=kCustom, calls=%fused_computation.5 | custom fusion | bytes 196800 | tf_op jit(solution)/shard_map/gather | solution.py:63
  144.6 0.0 copy-start.12
  144.7 0.0 slice-start.1
  144.7 15.4 %all_gather.7 = bf16[16,32,64,6]{1,2,3,0:T(8,128)(2,1)S(1)} all-gather(bf16[16,32,16,6]{1,2,3,0:T(8,128)(2,1)S(1)} %bitcast.101), channel_id=1, replica_groups=mesh['bus'=64,'harm'=4] {'harm'}, dimensions={2}, use_global_device_ids=true | all-gather | bytes 491520 | tf_op jit(solution)/shard_map/all_gather | solution.py:64
  160.1 1.0 copy.20
  161.2 0.8 fusion.47
  162.0 4.6 %collective-permute-start.9 = (bf16[16,32,6,16]{1,3,2,0:T(8,128)(2,1)S(1)}, bf16[16,32,6,16]{1,3,2,0:T(8,128)(2,1)S(1)}, u32[]{:S(2)}, u32[]{:S(2)}) collective-permute-start(bf16[16,32,6,16]{1,3,2,0:T(8,128)(2,1)S(1)} %fusion.47), channel_id=1, source_target_pairs={{4,0},{8,4},{12,8},{16,12},{20,16},{24,20},{28,24},{32,28},{36,32}... | collective-permute-start | bytes 294920 | tf_op jit(solution)/shard_map/ppermute | solution.py:19
  166.5 1.9 collective-permute-start.8
  168.5 0.1 broadcast_select_fusion
  168.6 1.4 fusion.35
  170.1 5.3 %collective-permute-done.9 = bf16[16,32,6,16]{1,3,2,0:T(8,128)(2,1)S(1)} collective-permute-done((bf16[16,32,6,16]{1,3,2,0:T(8,128)(2,1)S(1)}, bf16[16,32,6,16]{1,3,2,0:T(8,128)(2,1)S(1)}, u32[]{:S(2)}, u32[]{:S(2)}) %collective-permute-start.9) | collective-permute-done | bytes 98336 | tf_op jit(solution)/shard_map/ppermute | solution.py:19
  175.4 8.9 %collective-permute-done.8 = bf16[16,32,6,16]{1,3,2,0:T(8,128)(2,1)S(1)} collective-permute-done((bf16[16,32,6,16]{1,3,2,0:T(8,128)(2,1)S(1)}, bf16[16,32,6,16]{1,3,2,0:T(8,128)(2,1)S(1)}, u32[]{:S(2)}, u32[]{:S(2)}) %collective-permute-start.8) | collective-permute-done | bytes 98336 | tf_op jit(solution)/shard_map/ppermute | solution.py:17
  184.3 0.3 pad_maximum_fusion.3
  184.6 0.6 fusion.55
  185.2 1.4 copy.23
  186.5 1.8 reshape.64
  188.4 3.8 %fusion.51 = f32[16,3,32,128]{3,2,1,0:T(8,128)} fusion(bf16[16,3,128,128]{3,2,1,0:T(8,128)(2,1)S(1)} %copy-done, f32[16,3,32,128]{3,2,1,0:T(8,128)} %reshape.64, f32[16,3,32,128]{3,2,1,0:T(8,128)} %fusion.35, bf16[16,3,3,128,128]{4,3,2,1,0:T(8,128)(2,1)} %param.13, bf16[16,3,32,128]{3,2,1,0:T(8,128)(2,1)S(1)} %copy-done.1, ...), kind=kOutput, calls=%fused_computation.34 | convolution fusion | flops 101842944 | bytes 6291459 | tf_op jit(solution)/shard_map/htsa,htab->htsb/dot_general | solution.py:79
  (37 shorter events, 0.1 us)
Async XLA Ops:
  0.0 12.5 %copy-start = (bf16[16,3,128,128]{3,2,1,0:T(8,128)(2,1)S(1)}, bf16[16,3,128,128]{3,2,1,0:T(8,128)(2,1)}, u32[]{:S(2)}) copy-start(bf16[16,3,128,128]{3,2,1,0:T(8,128)(2,1)} %param.12) | copy-start | bytes 4718596
  0.0 24.6 %copy-start.4 = (s32[3,3]{1,0:T(4,128)S(1)}, s32[3,3]{1,0:T(4,128)}, u32[]{:S(2)}) copy-start(s32[3,3]{1,0:T(4,128)} %param.14) | copy-start | bytes 112
  1.5 25.4 %copy-start.5 = (s32[16]{0:T(128)S(1)}, s32[16]{0:T(128)}, u32[]{:S(2)}) copy-start(s32[16]{0:T(128)} %param.17) | copy-start | bytes 196
  1.5 25.4 %collective-permute-start.3 = (s32[16,2]{0,1:T(2,128)S(1)}, s32[16,2]{0,1:T(2,128)S(1)}, u32[]{:S(2)}, u32[]{:S(2)}) collective-permute-start(s32[16,2]{0,1:T(2,128)S(1)} %pad_add_fusion), channel_id=1, source_target_pairs={{4,0},{8,4},{12,8},{16,12},{20,16},{24,20},{28,24},{32,28},{36,32}... | collective-permute-start | bytes 392 | tf_op jit(solution)/shard_map/ppermute | solution.py:19
  10.5 16.4 %collective-permute-start.2 = (s32[16,2]{0,1:T(2,128)S(1)}, s32[16,2]{0,1:T(2,128)S(1)}, u32[]{:S(2)}, u32[]{:S(2)}) collective-permute-start(s32[16,2]{0,1:T(2,128)S(1)} %pad_add_fusion), channel_id=1, source_target_pairs={{0,4},{4,8},{8,12},{12,16},{16,20},{20,24},{24,28},{28,32},{32,36}... | collective-permute-start | bytes 392 | tf_op jit(solution)/shard_map/ppermute | solution.py:17
  14.0 16.5 %collective-permute-start.1 = (bf16[16,3,32,128]{3,2,1,0:T(8,128)(2,1)S(1)}, bf16[16,3,32,128]{3,2,1,0:T(8,128)(2,1)S(1)}, u32[]{:S(2)}, u32[]{:S(2)}) collective-permute-start(bf16[16,3,32,128]{3,2,1,0:T(8,128)(2,1)S(1)} %convolution_convert_fusion.1), channel_id=1, source_target_pairs={{4,0},{8,4},{12,8},{16,12},{20,16},{24,20},{28,24},{32,28},{36,32}... | collective-permute-start | bytes 1179656 | tf_op jit(solution)/shard_map/ppermute | solution.py:19
  22.7 16.8 %collective-permute-start = (bf16[16,3,32,128]{3,2,1,0:T(8,128)(2,1)S(1)}, bf16[16,3,32,128]{3,2,1,0:T(8,128)(2,1)}, u32[]{:S(2)}, u32[]{:S(2)}) collective-permute-start(bf16[16,3,32,128]{3,2,1,0:T(8,128)(2,1)S(1)} %convolution_convert_fusion.1), channel_id=1, source_target_pairs={{0,4},{4,8},{8,12},{12,16},{16,20},{20,24},{24,28},{28,32},{32,36}... | collective-permute-start | bytes 1179656 | tf_op jit(solution)/shard_map/ppermute | solution.py:17
  76.4 1.3 copy-start.11
  78.4 13.3 %collective-permute-start.5 = (bf16[16,32,6,16]{1,3,2,0:T(8,128)(2,1)S(1)}, bf16[16,32,6,16]{1,3,2,0:T(8,128)(2,1)S(1)}, u32[]{:S(2)}, u32[]{:S(2)}) collective-permute-start(bf16[16,32,6,16]{1,3,2,0:T(8,128)(2,1)S(1)} %fusion.44), channel_id=1, source_target_pairs={{4,0},{8,4},{12,8},{16,12},{20,16},{24,20},{28,24},{32,28},{36,32}... | collective-permute-start | bytes 294920 | tf_op jit(solution)/shard_map/ppermute | solution.py:19
  80.9 17.9 %collective-permute-start.4 = (bf16[16,32,6,16]{1,3,2,0:T(8,128)(2,1)S(1)}, bf16[16,32,6,16]{1,3,2,0:T(8,128)(2,1)}, u32[]{:S(2)}, u32[]{:S(2)}) collective-permute-start(bf16[16,32,6,16]{1,3,2,0:T(8,128)(2,1)S(1)} %fusion.44), channel_id=1, source_target_pairs={{0,4},{4,8},{8,12},{12,16},{16,20},{20,24},{24,28},{28,32},{32,36}... | collective-permute-start | bytes 294920 | tf_op jit(solution)/shard_map/ppermute | solution.py:17
  90.5 9.5 %copy-start.7 = (s32[48]{0:T(128)S(1)}, s32[48]{0:T(128)}, u32[]{:S(2)}) copy-start(s32[48]{0:T(128)} %slice_bitcast_fusion) | copy-start | bytes 580
  90.5 9.6 %copy-start.9 = (pred[48]{0:T(512)(128)(4,1)S(1)}, pred[48]{0:T(512)(128)(4,1)}, u32[]{:S(2)}) copy-start(pred[48]{0:T(512)(128)(4,1)} %compare_bitcast_fusion) | copy-start | bytes 148
  102.0 1.8 copy-start.1
  106.7 12.1 %collective-permute-start.7 = (bf16[16,3,32,128]{3,2,1,0:T(8,128)(2,1)S(1)}, bf16[16,3,32,128]{3,2,1,0:T(8,128)(2,1)S(1)}, u32[]{:S(2)}, u32[]{:S(2)}) collective-permute-start(bf16[16,3,32,128]{3,2,1,0:T(8,128)(2,1)S(1)} %convolution_convert_fusion), channel_id=1, source_target_pairs={{4,0},{8,4},{12,8},{16,12},{20,16},{24,20},{28,24},{32,28},{36,32}... | collective-permute-start | bytes 1179656 | tf_op jit(solution)/shard_map/ppermute | solution.py:19
  108.7 17.0 %collective-permute-start.6 = (bf16[16,3,32,128]{3,2,1,0:T(8,128)(2,1)S(1)}, bf16[16,3,32,128]{3,2,1,0:T(8,128)(2,1)}, u32[]{:S(2)}, u32[]{:S(2)}) collective-permute-start(bf16[16,3,32,128]{3,2,1,0:T(8,128)(2,1)S(1)} %convolution_convert_fusion), channel_id=1, source_target_pairs={{0,4},{4,8},{8,12},{12,16},{16,20},{20,24},{24,28},{28,32},{32,36}... | collective-permute-start | bytes 1179656 | tf_op jit(solution)/shard_map/ppermute | solution.py:17
  118.9 0.7 copy-start.3
  141.6 27.0 %slice-start = ((s8[4718592]{0:T(1024)(128)(4,1)}), s8[524288]{0:T(1024)(128)(4,1)S(1)}, s32[]{:S(2)}) async-start(s8[4718592]{0:T(1024)(128)(4,1)} %bitcast.90), calls=%async_computation | async-start | bytes 1048576
  144.6 16.5 %copy-start.12 = (bf16[16,6,16,384]{3,2,1,0:T(8,128)(2,1)S(1)}, bf16[16,6,16,384]{3,2,1,0:T(8,128)(2,1)}, u32[]{:S(2)}) copy-start(bf16[16,6,16,384]{3,2,1,0:T(8,128)(2,1)} %param.15) | copy-start | bytes 3538948
  144.7 23.9 %slice-start.1 = ((s8[4718592]{0:T(1024)(128)(4,1)}), s8[4194304]{0:T(1024)(128)(4,1)S(1)}, s32[]{:S(2)}) async-start(s8[4718592]{0:T(1024)(128)(4,1)} %bitcast.90), calls=%async_computation.1 | async-start | bytes 8388608
  161.2 7.3 %copy-start.2 = (bf16[6,16,32,128]{3,2,1,0:T(8,128)(2,1)S(1)}, bf16[6,16,32,128]{3,2,1,0:T(8,128)(2,1)}, u32[]{:S(2)}) copy-start(bf16[6,16,32,128]{3,2,1,0:T(8,128)(2,1)} %gather_fusion.5) | copy-start | bytes 2359300
  161.2 7.3 %copy-start.6 = (pred[6]{0:T(512)(128)(4,1)S(1)}, pred[6]{0:T(512)(128)(4,1)}, u32[]{:S(2)}) copy-start(pred[6]{0:T(512)(128)(4,1)} %compare_and_fusion.1) | copy-start | bytes 22
  162.0 13.4 %collective-permute-start.9 = (bf16[16,32,6,16]{1,3,2,0:T(8,128)(2,1)S(1)}, bf16[16,32,6,16]{1,3,2,0:T(8,128)(2,1)S(1)}, u32[]{:S(2)}, u32[]{:S(2)}) collective-permute-start(bf16[16,32,6,16]{1,3,2,0:T(8,128)(2,1)S(1)} %fusion.47), channel_id=1, source_target_pairs={{4,0},{8,4},{12,8},{16,12},{20,16},{24,20},{28,24},{32,28},{36,32}... | collective-permute-start | bytes 294920 | tf_op jit(solution)/shard_map/ppermute | solution.py:19
  166.5 17.8 %collective-permute-start.8 = (bf16[16,32,6,16]{1,3,2,0:T(8,128)(2,1)S(1)}, bf16[16,32,6,16]{1,3,2,0:T(8,128)(2,1)S(1)}, u32[]{:S(2)}, u32[]{:S(2)}) collective-permute-start(bf16[16,32,6,16]{1,3,2,0:T(8,128)(2,1)S(1)} %fusion.47), channel_id=1, source_target_pairs={{0,4},{4,8},{8,12},{12,16},{16,20},{20,24},{24,28},{28,32},{32,36}... | collective-permute-start | bytes 294920 | tf_op jit(solution)/shard_map/ppermute | solution.py:17
  170.1 14.5 %copy-start.8 = (s32[48]{0:T(128)S(1)}, s32[48]{0:T(128)}, u32[]{:S(2)}) copy-start(s32[48]{0:T(128)} %slice_bitcast_fusion) | copy-start | bytes 580
  170.1 14.5 %copy-start.10 = (pred[48]{0:T(512)(128)(4,1)S(1)}, pred[48]{0:T(512)(128)(4,1)}, u32[]{:S(2)}) copy-start(pred[48]{0:T(512)(128)(4,1)} %compare_bitcast_fusion) | copy-start | bytes 148
where the time goes:
time: 193 us; the launch traced here: 192 us
  local copies, waits for them, and re-layouts  48.1 us (25%)
  waiting for transfers between devices  45 us (23%)
  starting transfers between devices  39.8 us (21%)
  blocking collectives  35 us (18%)
  matrix products  15.8 us (8%)
  other arithmetic  8.15 us (4%)
    all_gather x2, blocking collectives, per_device(): piece = lax.all_gather(terminal, 'harm', axis=2, tiled=True)  35 us
    ppermute x5, waiting for transfers between devices, extended(): lax.ppermute(tail, axis, [(i, (i + 1) % count) for i in range(ends)])  31.1 us
    ppermute x5, starting transfers between devices, extended(): lax.ppermute(head, axis, [((i + 1) % count, i) for i in range(ends)])  26.7 us
    reshape x4, local copies, waits for them, and re-layouts, per_device(): window.reshape(harm_dev, 3, 3, blocks_dev, scenarios, 2, half)  26.2 us
    ppermute x5, waiting for transfers between devices, extended(): lax.ppermute(head, axis, [((i + 1) % count, i) for i in range(ends)])  13.9 us
    ppermute x5, starting transfers between devices, extended(): lax.ppermute(tail, axis, [(i, (i + 1) % count) for i in range(ends)])  13.1 us
    dot_general x2, matrix products, per_device(): jnp.einsum('htsa,htab->htsb', residual, inv_diag, preferred_element_type=...  6.78 us
    gather x4, local copies, waits for them, and re-layouts, per_device(): grid[own_shard, bus_block, bus_row]  6.04 us
  transfers between devices with their start and end apart: 10, of which 8 were waited for; matrix products, arithmetic and copies ran while one was open for 7% of the time, Pallas kernels for 0%

commit v1 on v0

v1 whole, which is shorter than its diff:
```python
import functools

import jax
import jax.numpy as jnp
import numpy as np
from jax import lax
from jax.experimental import pallas as pl
from jax.experimental.pallas import tpu as pltpu
from jax.sharding import PartitionSpec as P

ITERS = 2
MESH = pl.DeviceIdType.MESH
F32 = jnp.float32
BF16 = jnp.bfloat16

X_L, X_R, V_L, V_R, T_SIB, T_PAR, T_FWD, Z_L, Z_R = range(9)
PER_SWEEP = 9


def dot(a, b):
    return jnp.dot(a, b, preferred_element_type=F32)


def block_swap(a, masks):
    out = a
    for k in range(1, 4):
        moved = pltpu.roll(pltpu.roll(a, 32 * k, 1), 8 - 2 * k, 0)
        out = jnp.where(masks[k], moved, out)
    return out


def kernel(
    n_bus,
    site_ref, bus_ref, pat_ref, order_ref, inj_hbm, inv_hbm, off_hbm, cpl_hbm,
    out_hbm,
    inj, inv, off, cpl, perm, bp, vb, win_0, win_1, tabs, ehot, hh, base, xs, xr, tta, ttb, cur, zz, spread, outv,
    load_sem, send_sem, recv_sem, tab_send, tab_recv, out_sem,
):
    win = (win_0, win_1)
    me = lax.axis_index("bus")
    harm = lax.axis_index("harm")
    left = lax.rem(me + n_bus - 1, n_bus)
    right = lax.rem(me + 1, n_bus)
    zh, core = harm // 2, lax.rem(harm, 2)
    to_left, to_right = (left, harm), (right, harm)
    sibling = (me, zh * 2 + 1 - core)
    partner = (me, (1 - zh) * 2 + core)

    loads = [
        pltpu.make_async_copy(src, dst, load_sem.at[i])
        for i, (src, dst) in enumerate(((inj_hbm, inj), (inv_hbm, inv), (cpl_hbm, cpl), (off_hbm, off)))
    ]
    for load in loads:
        load.start()

    barrier = pltpu.get_barrier_semaphore()
    for peer in (to_left, to_right, sibling, partner):
        pl.semaphore_signal(barrier, inc=1, device_id=peer, device_id_type=MESH)

    conv_row = lax.broadcasted_iota(jnp.int32, (32, 128), 0) // 2
    table = jnp.zeros((32, 128), jnp.int32)
    for c in range(16):
        table = jnp.where(conv_row == c, site_ref[c] * 128 + bus_ref[c], table)
    tabs[1] = table

    pl.semaphore_wait(barrier, 4)

    def remote(src, dst, send, recv, peer):
        return pltpu.make_async_remote_copy(
            src_ref=src, dst_ref=dst, send_sem=send, recv_sem=recv, device_id=peer, device_id_type=MESH
        )

    tab_copies = [
        remote(tabs.at[1], tabs.at[0], tab_send.at[0], tab_recv.at[0], to_right),
        remote(tabs.at[1], tabs.at[2], tab_send.at[1], tab_recv.at[1], to_left),
    ]
    for copy in tab_copies:
        copy.start()

    def sweep_copies(w):
        def one(slot, src, dst, peer):
            return remote(src, dst, send_sem.at[w * PER_SWEEP + slot], recv_sem.at[w * PER_SWEEP + slot], peer)

        return [
            one(X_L, xs.at[w, 0], xr.at[w, 1], to_left),
            one(X_R, xs.at[w, 2], xr.at[w, 0], to_right),
            one(V_L, vb.at[w], win[w].at[2], to_left),
            one(V_R, vb.at[w], win[w].at[0], to_right),
            one(T_SIB, tta.at[w, pl.ds(0, 96)], tta.at[w, pl.ds(96, 96)], sibling),
            one(T_PAR, tta.at[w, pl.ds(0, 96)], ttb.at[w, pl.ds(0, 96)], partner),
            one(T_FWD, ttb.at[w, pl.ds(0, 96)], ttb.at[w, pl.ds(96, 96)], sibling),
            one(Z_L, zz.at[w, 1], zz.at[w, 2], to_left),
            one(Z_R, zz.at[w, 1], zz.at[w, 0], to_right),
        ]

    loads[0].wait()
    loads[1].wait()

    def first(h, carry):
        for p in range(3):
            rounded = dot(inj[h, p], inv[h, p]).astype(BF16)
            vb[0, h, p] = rounded
            win[0][1, h, p] = rounded
        return carry

    lax.fori_loop(0, 16, first, 0, unroll=4)

    for copy in tab_copies:
        copy.wait()

    parity = lax.rem(lax.broadcasted_iota(jnp.int32, (32, 128), 0), 2)
    lane = lax.broadcasted_iota(jnp.int32, (32, 128), 1)
    row256 = lax.rem(lax.broadcasted_iota(jnp.int32, (32, 256), 0), 2)
    lane256 = lax.broadcasted_iota(jnp.int32, (32, 256), 1)
    bus256 = lax.rem(lane256, 64) + me * 128
    part256 = lane256 // 64
    for g in range(3):
        tab = tabs[g]
        hit = (tab + parity * 64) == (lane + me * 128)
        ehot[g * 32 : g * 32 + 32] = jnp.where(hit, 1.0, 0.0).astype(BF16)
        wide = jnp.concatenate([tab, tab], axis=1)
        for m in range(2):
            hit = (wide == bus256) & (part256 == row256 * 2 + m)
            at = g * 64 + m * 32
            hh[at : at + 32] = jnp.where(hit, 1.0, 0.0).astype(BF16)

    sub = lax.broadcasted_iota(jnp.int32, (8, 128), 0) // 2
    chunk = lax.broadcasted_iota(jnp.int32, (8, 128), 1) // 32
    shift = lax.rem(chunk - sub + 4, 4)
    masks = [shift == k for k in range(4)]
    chunk96 = lax.broadcasted_iota(jnp.int32, (96, 128), 1) // 32
    chunk_masks = [chunk96 == k for k in range(4)]

    links = []
    for p in range(3):
        at = [pat_ref[p, k] - (me - 1) * 3 for k in range(3)]
        own = [(a >= 3) & (a < 6) for a in at]
        k0 = jnp.where(own[0], 0, jnp.where(own[1], 1, 2))
        k1 = jnp.where(k0 == 0, 1, 0)
        k2 = jnp.where(k0 == 2, 1, 2)

        def pick(k):
            return jnp.where(k == 0, at[0], jnp.where(k == 1, at[1], at[2]))

        links.append((k0, jnp.clip(pick(k0) - 3, 0, 2), k1, jnp.clip(pick(k1), 0, 8), k2, jnp.clip(pick(k2), 0, 8)))

    for w in range(ITERS):
        copies = sweep_copies(w)
        for j in range(6):
            some = vb[w].reshape(1536, 128)[j * 256 : j * 256 + 256]
            got = lax.dot_general(
                ehot[...], some, (((1,), (1,)), ((), ())), preferred_element_type=F32
            ).astype(BF16)
            for g in range(3):
                xs[w, g, :, j * 256 : j * 256 + 256] = got[g * 32 : g * 32 + 32]
        for slot in (X_L, X_R, V_L, V_R):
            copies[slot].start()

        if w == 0:
            loads[2].wait()
            col = lax.broadcasted_iota(jnp.int32, (8, 512), 1)
            slot_bits = (col // 256) * 2 + jnp.where(lax.rem(col, 256) >= 96, 1, 0)
            source = jnp.bitwise_xor(slot_bits, harm) * 96 + order_ref[...]
            for r in range(48):
                row = lax.broadcasted_iota(jnp.int32, (8, 512), 0) + r * 8
                hot = jnp.where(row == source[0:1], 1.0, 0.0)
                if r % 2 == 0:
                    kept = hot
                else:
                    perm[(r - 1) * 8 : (r + 1) * 8] = jnp.concatenate([kept, hot], axis=0).astype(BF16)

            def permute(c, carry):
                rows = pl.ds(pl.multiple_of(c * 96, 96), 96)
                bp[rows] = dot(cpl[rows], perm[...]).astype(BF16)
                return carry

            lax.fori_loop(0, 16, permute, 0)

        copies[X_L].wait_recv()
        copies[X_R].wait_recv()
        for tp in range(6):
            for up in range(2):
                both = []
                for t in (2 * tp, 2 * tp + 1):
                    rows, lanes = slice(up * 16, up * 16 + 16), slice(t * 128, t * 128 + 128)
                    both.append(
                        xs[w, 1, rows, lanes].astype(F32)
                        + xr[w, 0, rows, lanes].astype(F32)
                        + xr[w, 1, rows, lanes].astype(F32)
                    )
                for half in range(2):
                    u = up * 2 + half
                    swapped = [block_swap(b[half * 8 : half * 8 + 8], masks) for b in both]
                    tta[w, tp * 16 : tp * 16 + 16, u * 128 : u * 128 + 128] = jnp.concatenate(
                        swapped, axis=0
                    ).astype(BF16)
        copies[T_PAR].start()
        copies[T_SIB].start()

        if w == 0:
            loads[3].wait()

        def own_links(h, carry):
            for p in range(3):
                k0, own_at = links[p][:2]
                base[h, p] = inj[h, p].astype(F32) - dot(vb[w, h, own_at], off[h, p, k0])
            return carry

        lax.fori_loop(0, 16, own_links, 0, unroll=4)

        def couple(held, at, add):
            for u in range(4):
                rhs = held[w, :, u * 128 : u * 128 + 128]
                total = None
                for q in range(4):
                    c = u * 4 + q
                    one = dot(bp[c * 96 : c * 96 + 96, at : at + 192], rhs)
                    total = one if total is None else jnp.where(chunk_masks[q], one, total)
                lanes = slice(u * 128, u * 128 + 128)
                cur[:, lanes] = cur[:, lanes] + total if add else total

        copies[T_SIB].wait_recv()
        couple(tta, 0, False)
        copies[T_PAR].wait_recv()
        copies[T_FWD].start()
        copies[T_FWD].wait_recv()
        couple(ttb, 256, True)

        for up in range(2):
            for j in range(12):
                m, ph = j // 6, j % 6
                swapped = [
                    block_swap(cur[j * 8 : j * 8 + 8, u * 128 : u * 128 + 128], masks)
                    for u in (2 * up, 2 * up + 1)
                ]
                at = m * 32 + up * 16
                zz[w, 1, at : at + 16, ph * 128 : ph * 128 + 128] = jnp.concatenate(
                    swapped, axis=0
                ).astype(BF16)
        copies[Z_L].start()
        copies[Z_R].start()

        copies[V_L].wait_recv()
        copies[V_R].wait_recv()

        def other_links(h, carry):
            for p in range(3):
                _, _, k1, at1, k2, at2 = links[p]
                columns = jnp.concatenate(
                    [win[w][at1 // 3, h, lax.rem(at1, 3)], win[w][at2 // 3, h, lax.rem(at2, 3)]], axis=1
                )
                tiles = jnp.concatenate([off[h, p, k1], off[h, p, k2]], axis=0)
                base[h, p] = base[h, p] - dot(columns, tiles)
            return carry

        lax.fori_loop(0, 16, other_links, 0, unroll=4)

        copies[Z_L].wait_recv()
        copies[Z_R].wait_recv()
        spread[...] = lax.dot_general(
            zz[w].reshape(192, 768), hh[...], (((0,), (0,)), ((), ())), preferred_element_type=F32
        )

        def finish(hq, carry):
            for p in range(3):
                rows = pl.ds(pl.multiple_of(p * 256 + hq * 32, 32), 32)
                for e in range(2):
                    h = hq * 2 + e
                    residual = (base[h, p] - spread[rows, e * 128 : e * 128 + 128]).astype(BF16)
                    voltage = dot(residual, inv[h, p])
                    if w == ITERS - 1:
                        outv[h, p] = voltage
                    else:
                        rounded = voltage.astype(BF16)
                        vb[w + 1, h, p] = rounded
                        win[w + 1][1, h, p] = rounded
            return carry

        lax.fori_loop(0, 8, finish, 0, unroll=2)

    result = pltpu.make_async_copy(outv, out_hbm, out_sem)
    result.start()
    for w in range(ITERS):
        for copy in sweep_copies(w):
            copy.wait_send()
    result.wait()


def column_order():
    order = np.full((512,), -100000, np.int32)
    for pair in range(2):
        for slot in range(2):
            for h in range(16):
                for p in range(3):
                    for m in range(2):
                        order[pair * 256 + slot * 96 + h * 6 + p * 2 + m] = h * 6 + m * 3 + p
    return np.tile(order[None], (8, 1))


def per_device(n_bus, injection, inv_diag, off_tiles, pattern, coupling, site_map, bus_map):
    smem = pl.BlockSpec(memory_space=pltpu.SMEM)
    hbm = pl.BlockSpec(memory_space=pl.ANY)
    vmem = pl.BlockSpec(memory_space=pltpu.VMEM)
    dma = pltpu.SemaphoreType.DMA
    tiles = (16, 3, 32, 128)
    return pl.pallas_call(
        functools.partial(kernel, n_bus),
        out_shape=jax.ShapeDtypeStruct(tiles, F32),
        in_specs=[smem, smem, smem, vmem, hbm, hbm, hbm, hbm],
        out_specs=hbm,
        scratch_shapes=[
            pltpu.VMEM(tiles, BF16),
            pltpu.VMEM((16, 3, 128, 128), BF16),
            pltpu.VMEM((16, 3, 3, 128, 128), BF16),
            pltpu.VMEM((1536, 384), BF16),
            pltpu.VMEM((384, 512), BF16),
            pltpu.VMEM((1536, 512), BF16),
            pltpu.VMEM((ITERS,) + tiles, BF16),
            pltpu.VMEM((3,) + tiles, BF16),
            pltpu.VMEM((3,) + tiles, BF16),
            pltpu.VMEM((3, 32, 128), jnp.int32),
            pltpu.VMEM((96, 128), BF16),
            pltpu.VMEM((192, 256), BF16),
            pltpu.VMEM(tiles, F32),
            pltpu.VMEM((ITERS, 3, 32, 1536), BF16),
            pltpu.VMEM((ITERS, 2, 32, 1536), BF16),
            pltpu.VMEM((ITERS, 192, 512), BF16),
            pltpu.VMEM((ITERS, 192, 512), BF16),
            pltpu.VMEM((96, 512), F32),
            pltpu.VMEM((ITERS, 3, 64, 768), BF16),
            pltpu.VMEM((768, 256), F32),
            pltpu.VMEM(tiles, F32),
            dma((4,)),
            dma((ITERS * PER_SWEEP,)),
            dma((ITERS * PER_SWEEP,)),
            dma((2,)),
            dma((2,)),
            dma,
        ],
        compiler_params=pltpu.CompilerParams(
            collective_id=0, has_side_effects=True, vmem_limit_bytes=56 << 20
        ),
    )(
        site_map,
        bus_map,
        pattern,
        jnp.asarray(column_order()),
        injection,
        inv_diag,
        off_tiles,
        coupling.reshape(1536, 384),
    )


def solution(mesh):
    in_specs = (
        P("harm", "bus", None, None),
        P("harm", "bus", None, None),
        P("harm", "bus", None, None, None),
        P("bus", None),
        P("bus", None, "harm", None),
        P("bus"),
        P("bus"),
    )
    out_specs = P("harm", "bus", None, None)
    return jax.shard_map(
        functools.partial(per_device, mesh.shape["bus"]),
        mesh=mesh,
        in_specs=in_specs,
        out_specs=out_specs,
        check_vma=False,
    )
```

time: 193 us -> 76.4 us (0.40)
  the two profiles are of different devices: /device:TPU:24 before, /device:TPU:1 now
where the time goes in v1:
time: 76.4 us; the launch traced here: 76.2 us
  Pallas kernels  74.1 us (97%)
  local copies, waits for them, and re-layouts  2.07 us (3%)
    pallas_call x1, Pallas kernels, per_device(): pl.pallas_call(functools.partial(kernel, n_bus), out_shape=jax.ShapeDtype...  74.1 us
    unnamed x1, local copies, waits for them, and re-layouts  2.07 us

profile of v1, /device:TPU:1, one launch (start us, length us, event | category | flops | bytes accessed | tf_op | source)
XLA Modules:
  0.0 76.2 jit_solution(18292853590032494121)
XLA Ops:
  0.0 74.1 %shard_map.82 = f32[16,3,32,128]{3,2,1,0:T(8,128)} custom-call(s32[16]{0:T(128)} %site_ref.1, s32[16]{0:T(128)} %bus_ref.1, s32[3,3]{1,0:T(4,128)} %pat_ref.1, s32[8,512]{1,0:T(8,128)} %constant.2.clone.order_ref, bf16[16,3,32,128]{3,2,1,0:T(8,128)(2,1)} %inj_hbm.1, bf16[16,3,128,128]{3,2,1,0:T(8,128)(2,1)} %inv_hbm.1, ...), custom_call_target="tpu_custom_call" | custom-call | tf_op jit(solution)/shard_map/pallas_call | solution.py:306
  74.1 2.1 %copy.10 = f32[16,3,32,128]{3,2,1,0:T(8,128)} copy(f32[16,3,32,128]{3,2,1,0:T(8,128)} %shard_map.82) | data formatting | bytes 1572864

commit v2 on v1

v2 whole, which is shorter than its diff:
```python
import functools

import jax
import jax.numpy as jnp
import numpy as np
from jax import lax
from jax.experimental import pallas as pl
from jax.experimental.pallas import tpu as pltpu
from jax.sharding import PartitionSpec as P

ITERS = 2
MESH = pl.DeviceIdType.MESH
F32 = jnp.float32
BF16 = jnp.bfloat16

V_RUNS = ((0, 6), (6, 11), (11, 16))
T_RUNS = ((0, 64), (64, 96))
T_AFTER = (1, 2)


def dot(a, b):
    return jnp.dot(a, b, preferred_element_type=F32)


def block_swap(a, masks):
    out = a
    for k in range(1, 4):
        moved = pltpu.roll(pltpu.roll(a, 32 * k, 1), 8 - 2 * k, 0)
        out = jnp.where(masks[k], moved, out)
    return out


def kernel(
    n_bus,
    site_ref, bus_ref, pat_ref, order_ref, inj_hbm, inv_hbm, off_hbm, cpl_hbm,
    out_hbm,
    inj, inv, off, cpl, perm, bp, vb, win_0, win_1, tabs, ehot, hh, base, xs, tta, ttb, cur, zz, spread, resid,
    load_sem, v_send, v_recv, t_send, t_recv, f_send, f_recv, s_send, s_recv, z_send, z_recv, tab_send, tab_recv, out_sem,
):
    win = (win_0, win_1)
    me = lax.axis_index("bus")
    harm = lax.axis_index("harm")
    left = lax.rem(me + n_bus - 1, n_bus)
    right = lax.rem(me + 1, n_bus)
    zh, core = harm // 2, lax.rem(harm, 2)
    to_left, to_right = (left, harm), (right, harm)
    sibling = (me, zh * 2 + 1 - core)
    partner = (me, (1 - zh) * 2 + core)

    loads = [
        pltpu.make_async_copy(src, dst, load_sem.at[i])
        for i, (src, dst) in enumerate(((inj_hbm, inj), (inv_hbm, inv), (cpl_hbm, cpl), (off_hbm, off)))
    ]
    for load in loads:
        load.start()

    barrier = pltpu.get_barrier_semaphore()
    for peer in (to_left, to_right, sibling, partner):
        pl.semaphore_signal(barrier, inc=1, device_id=peer, device_id_type=MESH)

    def remote(src, dst, send, recv, peer):
        return pltpu.make_async_remote_copy(
            src_ref=src, dst_ref=dst, send_sem=send, recv_sem=recv, device_id=peer, device_id_type=MESH
        )

    tab_copies = [
        remote(tabs.at[1], tabs.at[0], tab_send.at[0], tab_recv.at[0], to_right),
        remote(tabs.at[1], tabs.at[2], tab_send.at[1], tab_recv.at[1], to_left),
    ]

    def v_copies(w, j):
        run = pl.ds(V_RUNS[j][0], V_RUNS[j][1] - V_RUNS[j][0])
        return [
            remote(vb.at[w, run], win[w].at[2, run], v_send.at[w, j, 0], v_recv.at[w, j, 0], to_left),
            remote(vb.at[w, run], win[w].at[0, run], v_send.at[w, j, 1], v_recv.at[w, j, 1], to_right),
        ]

    def rows_of(i, at):
        return pl.ds(at + T_RUNS[i][0], T_RUNS[i][1] - T_RUNS[i][0])

    def t_copy(w, i):
        return remote(
            tta.at[w, rows_of(i, 0)], ttb.at[w, rows_of(i, 0)], t_send.at[w, i], t_recv.at[w, i], partner
        )

    def f_copy(w, i):
        return remote(
            ttb.at[w, rows_of(i, 0)], ttb.at[w, rows_of(i, 96)], f_send.at[w, i], f_recv.at[w, i], sibling
        )

    def s_copy(w):
        return remote(tta.at[w, pl.ds(0, 96)], tta.at[w, pl.ds(96, 96)], s_send.at[w], s_recv.at[w], sibling)

    def z_copies(w):
        return [
            remote(zz.at[w, 1], zz.at[w, 2], z_send.at[w, 0], z_recv.at[w, 0], to_left),
            remote(zz.at[w, 1], zz.at[w, 0], z_send.at[w, 1], z_recv.at[w, 1], to_right),
        ]

    conv_row = lax.broadcasted_iota(jnp.int32, (32, 128), 0) // 2
    table = jnp.zeros((32, 128), jnp.int32)
    for c in range(16):
        table = jnp.where(conv_row == c, site_ref[c] * 128 + bus_ref[c], table)
    tabs[1] = table
    parity = lax.rem(lax.broadcasted_iota(jnp.int32, (32, 128), 0), 2)
    lane = lax.broadcasted_iota(jnp.int32, (32, 128), 1)
    for g in range(3):
        hit = (table + parity * 64) == (lane + (me - 1 + g) * 128)
        ehot[:, g * 128 : g * 128 + 128] = jnp.where(hit, 1.0, 0.0).astype(BF16)

    loads[0].wait()
    loads[1].wait()

    def first(h, carry):
        for p in range(3):
            rounded = dot(inj[h, p], inv[h, p]).astype(BF16)
            vb[0, h, p] = rounded
            win[0][1, h, p] = rounded
        return carry

    lax.fori_loop(0, 16, first, 0, unroll=4)

    pl.semaphore_wait(barrier, 4)
    for j in range(len(V_RUNS)):
        for copy in v_copies(0, j):
            copy.start()
    for copy in tab_copies:
        copy.start()

    sub = lax.broadcasted_iota(jnp.int32, (8, 128), 0) // 2
    chunk = lax.broadcasted_iota(jnp.int32, (8, 128), 1) // 32
    shift = lax.rem(chunk - sub + 4, 4)
    masks = [shift == k for k in range(4)]
    chunk96 = lax.broadcasted_iota(jnp.int32, (96, 128), 1) // 32
    chunk_masks = [chunk96 == k for k in range(4)]

    links = []
    for p in range(3):
        at = [pat_ref[p, k] - (me - 1) * 3 for k in range(3)]
        own = [(a >= 3) & (a < 6) for a in at]
        k0 = jnp.where(own[0], 0, jnp.where(own[1], 1, 2))
        k1 = jnp.where(k0 == 0, 1, 0)
        k2 = jnp.where(k0 == 2, 1, 2)

        def pick(k):
            return jnp.where(k == 0, at[0], jnp.where(k == 1, at[1], at[2]))

        links.append((k0, jnp.clip(pick(k0) - 3, 0, 2), k1, jnp.clip(pick(k1), 0, 8), k2, jnp.clip(pick(k2), 0, 8)))

    col = lax.broadcasted_iota(jnp.int32, (8, 512), 1)
    slot_bits = jnp.where(col < 256, jnp.where(col >= 96, 1, 0), jnp.where(col >= 384, 3, 2))
    source = jnp.bitwise_xor(slot_bits, harm) * 96 + order_ref[...]
    for r in range(48):
        row = lax.broadcasted_iota(jnp.int32, (8, 512), 0) + r * 8
        hot = jnp.where(row == source[0:1], 1.0, 0.0)
        if r % 2 == 0:
            kept = hot
        else:
            perm[(r - 1) * 8 : (r + 1) * 8] = jnp.concatenate([kept, hot], axis=0).astype(BF16)
    loads[2].wait()

    def permute(c, carry):
        rows = pl.ds(pl.multiple_of(c * 96, 96), 96)
        bp[rows] = dot(cpl[rows], perm[...]).astype(BF16)
        return carry

    lax.fori_loop(0, 16, permute, 0)
    loads[3].wait()

    for w in range(ITERS):

        def own_links(h, carry):
            for p in range(3):
                k0, own_at = links[p][:2]
                base[h, p] = inj[h, p].astype(F32) - dot(vb[w, h, own_at], off[h, p, k0])
            return carry

        lax.fori_loop(0, 16, own_links, 0, unroll=4)

        sent = 0
        for j, (start, stop) in enumerate(V_RUNS):
            for copy in v_copies(w, j):
                copy.wait_recv()
            count = (stop - start) * 96
            held = jnp.concatenate(
                [win[w][g, start:stop].reshape(count, 128) for g in range(3)], axis=1
            )
            xs[:, start * 96 : stop * 96] = lax.dot_general(
                ehot[...], held, (((1,), (1,)), ((), ())), preferred_element_type=F32
            )
            while sent < len(T_RUNS) and T_AFTER[sent] == j:
                for tp in range(T_RUNS[sent][0] // 16, T_RUNS[sent][1] // 16):
                    for u in range(4):
                        swapped = [
                            block_swap(xs[u * 8 : u * 8 + 8, t * 128 : t * 128 + 128], masks)
                            for t in (2 * tp, 2 * tp + 1)
                        ]
                        tta[w, tp * 16 : tp * 16 + 16, u * 128 : u * 128 + 128] = jnp.concatenate(
                            swapped, axis=0
                        ).astype(BF16)
                t_copy(w, sent).start()
                sent += 1
        s_copy(w).start()

        if w == 0:
            for copy in tab_copies:
                copy.wait()
            row256 = lax.rem(lax.broadcasted_iota(jnp.int32, (32, 256), 0), 2)
            lane256 = lax.broadcasted_iota(jnp.int32, (32, 256), 1)
            bus256 = lax.rem(lane256, 64) + me * 128
            part256 = lane256 // 64
            for g in range(3):
                wide = jnp.concatenate([tabs[g], tabs[g]], axis=1)
                for m in range(2):
                    hit = (wide == bus256) & (part256 == row256 * 2 + m)
                    at = g * 64 + m * 32
                    hh[at : at + 32] = jnp.where(hit, 1.0, 0.0).astype(BF16)

        def other_links(h, carry):
            for p in range(3):
                _, _, k1, at1, k2, at2 = links[p]
                columns = jnp.concatenate(
                    [win[w][at1 // 3, h, lax.rem(at1, 3)], win[w][at2 // 3, h, lax.rem(at2, 3)]], axis=1
                )
                tiles = jnp.concatenate([off[h, p, k1], off[h, p, k2]], axis=0)
                base[h, p] = base[h, p] - dot(columns, tiles)
            return carry

        lax.fori_loop(0, 16, other_links, 0, unroll=4)

        def couple(held, top, rows, at, add):
            for u in range(4):
                rhs = held[w, top : top + rows, u * 128 : u * 128 + 128]
                total = None
                for q in range(4):
                    c = u * 4 + q
                    one = dot(bp[c * 96 : c * 96 + 96, at : at + rows], rhs)
                    total = one if total is None else jnp.where(chunk_masks[q], one, total)
                lanes = slice(u * 128, u * 128 + 128)
                cur[:, lanes] = cur[:, lanes] + total if add else total

        s_copy(w).wait_recv()
        couple(tta, 0, 192, 0, False)
        for i in range(len(T_RUNS)):
            t_copy(w, i).wait_recv()
            f_copy(w, i).start()
        couple(ttb, 0, 96, 256, True)
        for i in range(len(T_RUNS)):
            f_copy(w, i).wait_recv()
        couple(ttb, 96, 96, 384, True)

        for up in range(2):
            for j in range(12):
                m, ph = j // 6, j % 6
                swapped = [
                    block_swap(cur[j * 8 : j * 8 + 8, u * 128 : u * 128 + 128], masks)
                    for u in (2 * up, 2 * up + 1)
                ]
                at = m * 32 + up * 16
                zz[w, 1, at : at + 16, ph * 128 : ph * 128 + 128] = jnp.concatenate(
                    swapped, axis=0
                ).astype(BF16)
        for copy in z_copies(w):
            copy.start()
        for copy in z_copies(w):
            copy.wait_recv()
        spread[...] = lax.dot_general(
            zz[w].reshape(192, 768), hh[...], (((0,), (0,)), ((), ())), preferred_element_type=F32
        )

        def finish(h, carry):
            hq, e = h // 2, lax.rem(h, 2)
            for p in range(3):
                rows = pl.ds(pl.multiple_of(p * 256 + hq * 32, 32), 32)
                lanes = pl.ds(pl.multiple_of(e * 128, 128), 128)
                residual = (base[h, p] - spread[rows, lanes]).astype(BF16)
                if w == ITERS - 1:
                    resid[h, p] = residual
                else:
                    rounded = dot(residual, inv[h, p]).astype(BF16)
                    vb[w + 1, h, p] = rounded
                    win[w + 1][1, h, p] = rounded
            return carry

        if w < ITERS - 1:
            for j, (start, stop) in enumerate(V_RUNS):
                lax.fori_loop(start, stop, finish, 0, unroll=stop - start)
                for copy in v_copies(w + 1, j):
                    copy.start()
        else:
            lax.fori_loop(0, 16, finish, 0, unroll=4)

    result = pltpu.make_async_copy(resid, out_hbm, out_sem)
    result.start()
    for w in range(ITERS):
        for j in range(len(V_RUNS)):
            for copy in v_copies(w, j):
                copy.wait_send()
        for i in range(len(T_RUNS)):
            t_copy(w, i).wait_send()
            f_copy(w, i).wait_send()
        s_copy(w).wait_send()
        for copy in z_copies(w):
            copy.wait_send()
    result.wait()


def column_order():
    order = np.full((512,), -100000, np.int32)
    for start in (0, 96, 256, 384):
        for h in range(16):
            for p in range(3):
                for m in range(2):
                    order[start + h * 6 + p * 2 + m] = h * 6 + m * 3 + p
    return np.tile(order[None], (8, 1))


def per_device(n_bus, injection, inv_diag, off_tiles, pattern, coupling, site_map, bus_map):
    smem = pl.BlockSpec(memory_space=pltpu.SMEM)
    hbm = pl.BlockSpec(memory_space=pl.ANY)
    vmem = pl.BlockSpec(memory_space=pltpu.VMEM)
    dma = pltpu.SemaphoreType.DMA
    tiles = (16, 3, 32, 128)
    runs, parts = len(V_RUNS), len(T_RUNS)
    residual = pl.pallas_call(
        functools.partial(kernel, n_bus),
        out_shape=jax.ShapeDtypeStruct(tiles, BF16),
        in_specs=[smem, smem, smem, vmem, hbm, hbm, hbm, hbm],
        out_specs=hbm,
        scratch_shapes=[
            pltpu.VMEM(tiles, BF16),
            pltpu.VMEM((16, 3, 128, 128), BF16),
            pltpu.VMEM((16, 3, 3, 128, 128), BF16),
            pltpu.VMEM((1536, 384), BF16),
            pltpu.VMEM((384, 512), BF16),
            pltpu.VMEM((1536, 512), BF16),
            pltpu.VMEM((ITERS,) + tiles, BF16),
            pltpu.VMEM((3,) + tiles, BF16),
            pltpu.VMEM((3,) + tiles, BF16),
            pltpu.VMEM((3, 32, 128), jnp.int32),
            pltpu.VMEM((32, 384), BF16),
            pltpu.VMEM((192, 256), BF16),
            pltpu.VMEM(tiles, F32),
            pltpu.VMEM((32, 1536), F32),
            pltpu.VMEM((ITERS, 192, 512), BF16),
            pltpu.VMEM((ITERS, 192, 512), BF16),
            pltpu.VMEM((96, 512), F32),
            pltpu.VMEM((ITERS, 3, 64, 768), BF16),
            pltpu.VMEM((768, 256), F32),
            pltpu.VMEM(tiles, BF16),
            dma((4,)),
            dma((ITERS, runs, 2)),
            dma((ITERS, runs, 2)),
            dma((ITERS, parts)),
            dma((ITERS, parts)),
            dma((ITERS, parts)),
            dma((ITERS, parts)),
            dma((ITERS,)),
            dma((ITERS,)),
            dma((ITERS, 2)),
            dma((ITERS, 2)),
            dma((2,)),
            dma((2,)),
            dma,
        ],
        compiler_params=pltpu.CompilerParams(
            collective_id=0, has_side_effects=True, vmem_limit_bytes=56 << 20
        ),
    )(
        site_map,
        bus_map,
        pattern,
        jnp.asarray(column_order()),
        injection,
        inv_diag,
        off_tiles,
        coupling.reshape(1536, 384),
    )
    return jnp.einsum("htsa,htab->htsb", residual, inv_diag, preferred_element_type=F32)


def solution(mesh):
    in_specs = (
        P("harm", "bus", None, None),
        P("harm", "bus", None, None),
        P("harm", "bus", None, None, None),
        P("bus", None),
        P("bus", None, "harm", None),
        P("bus"),
        P("bus"),
    )
    out_specs = P("harm", "bus", None, None)
    return jax.shard_map(
        functools.partial(per_device, mesh.shape["bus"]),
        mesh=mesh,
        in_specs=in_specs,
        out_specs=out_specs,
        check_vma=False,
    )
```

time: 76.4 us -> 69.5 us (0.910)
  Pallas kernels: 74.1 us -> 67 us
  matrix products: 0 us -> 2.4 us
  local copies, waits for them, and re-layouts: 2.07 us -> 0.01 us
    pallas_call x1, Pallas kernels: 74.1 us -> 67 us  [per_device(): pl.pallas_call(functools.partial(kernel, n_bus), out_shape=jax.ShapeDtype...]
    dot_general x0 -> x1, matrix products: none -> 2.4 us  [per_device(): jnp.einsum('htsa,htab->htsb', residual, inv_diag, preferred_element_type=...]
    unnamed x1 -> x2, local copies, waits for them, and re-layouts: 2.07 us -> 0.01 us
where the time goes in v2:
time: 69.5 us; the launch traced here: 69.4 us
  Pallas kernels  67 us (96%)
  matrix products  2.4 us (3%)
    pallas_call x1, Pallas kernels, per_device(): pl.pallas_call(functools.partial(kernel, n_bus), out_shape=jax.ShapeDtype...  67 us
    dot_general x1, matrix products, per_device(): jnp.einsum('htsa,htab->htsb', residual, inv_diag, preferred_element_type=...  2.4 us

profile of v2, /device:TPU:1, one launch (start us, length us, event | category | flops | bytes accessed | tf_op | source)
XLA Modules:
  0.0 69.4 jit_solution(15015560739743530339)
XLA Ops:
  0.0 0.0 copy-start
  0.0 67.0 %shard_map.82 = bf16[16,3,32,128]{3,2,1,0:T(8,128)(2,1)} custom-call(s32[16]{0:T(128)} %site_ref.1, s32[16]{0:T(128)} %bus_ref.1, s32[3,3]{1,0:T(4,128)} %pat_ref.1, s32[8,512]{1,0:T(8,128)} %constant.2.clone.order_ref, bf16[16,3,32,128]{3,2,1,0:T(8,128)(2,1)} %inj_hbm.1, bf16[16,3,128,128]{3,2,1,0:T(8,128)(2,1)} %inv_hbm.1, ...), custom_call_target="tpu_custom_call" | custom-call | tf_op jit(solution)/shard_map/pallas_call | solution.py:325
  67.0 0.0 copy-done
  67.0 2.4 %fusion = f32[16,3,32,128]{3,2,1,0:T(8,128)} fusion(bf16[16,3,32,128]{3,2,1,0:T(8,128)(2,1)} %shard_map.82, bf16[16,3,128,128]{3,2,1,0:T(8,128)(2,1)S(1)} %copy-done), kind=kOutput, calls=%fused_computation | convolution fusion | flops 50331648 | bytes 2752512 | tf_op jit(solution)/shard_map/htsa,htab->htsb/dot_general | solution.py:379
Async XLA Ops:
  0.0 67.0 %copy-start = (bf16[16,3,128,128]{3,2,1,0:T(8,128)(2,1)S(1)}, bf16[16,3,128,128]{3,2,1,0:T(8,128)(2,1)}, u32[]{:S(2)}) copy-start(bf16[16,3,128,128]{3,2,1,0:T(8,128)(2,1)} %inv_hbm.1) | copy-start | bytes 4718596

commit v3 on v2

--- a/solution.py
+++ b/solution.py
@@ -13,9 +13,9 @@
 F32 = jnp.float32
 BF16 = jnp.bfloat16
 
-V_RUNS = ((0, 6), (6, 11), (11, 16))
-T_RUNS = ((0, 64), (64, 96))
-T_AFTER = (1, 2)
+V_RUNS = ((0, 8), (8, 16))
+HALF_ROWS = 48
+DIRECT = ()
 
 
 def dot(a, b):
@@ -34,8 +34,8 @@
     n_bus,
     site_ref, bus_ref, pat_ref, order_ref, inj_hbm, inv_hbm, off_hbm, cpl_hbm,
     out_hbm,
-    inj, inv, off, cpl, perm, bp, vb, win_0, win_1, tabs, ehot, hh, base, xs, tta, ttb, cur, zz, spread, resid,
-    load_sem, v_send, v_recv, t_send, t_recv, f_send, f_recv, s_send, s_recv, z_send, z_recv, tab_send, tab_recv, out_sem,
+    inj, inv, off, cpl, perm, bp, vb, win_0, win_1, tabs, ehot, hh, base, xs, xr, tta, ttb, cur, zz, spread, resid,
+    load_sem, v_send, v_recv, x_send, x_recv, t_send, t_recv, f_send, f_recv, s_send, s_recv, z_send, z_recv, tab_send, tab_recv, out_sem,
 ):
     win = (win_0, win_1)
     me = lax.axis_index("bus")
@@ -46,6 +46,7 @@
     to_left, to_right = (left, harm), (right, harm)
     sibling = (me, zh * 2 + 1 - core)
     partner = (me, (1 - zh) * 2 + core)
+    across = (me, (1 - zh) * 2 + 1 - core)
 
     loads = [
         pltpu.make_async_copy(src, dst, load_sem.at[i])
@@ -55,7 +56,7 @@
         load.start()
 
     barrier = pltpu.get_barrier_semaphore()
-    for peer in (to_left, to_right, sibling, partner):
+    for peer in (to_left, to_right, sibling, partner, across):
         pl.semaphore_signal(barrier, inc=1, device_id=peer, device_id_type=MESH)
 
     def remote(src, dst, send, recv, peer):
@@ -75,26 +76,38 @@
             remote(vb.at[w, run], win[w].at[0, run], v_send.at[w, j, 1], v_recv.at[w, j, 1], to_right),
         ]
 
-    def rows_of(i, at):
-        return pl.ds(at + T_RUNS[i][0], T_RUNS[i][1] - T_RUNS[i][0])
-
-    def t_copy(w, i):
+    def x_copies(w, j):
+        lanes = pl.ds(j * 768, 768)
+        return [
+            remote(xs.at[w, 0, :, lanes], xr.at[w, 1, :, lanes], x_send.at[w, j, 0], x_recv.at[w, j, 0], to_left),
+            remote(xs.at[w, 2, :, lanes], xr.at[w, 0, :, lanes], x_send.at[w, j, 1], x_recv.at[w, j, 1], to_right),
+        ]
+
+    def rows_of(j, at):
+        return pl.ds(at + j * HALF_ROWS, HALF_ROWS)
+
+    def t_copy(w, j):
         return remote(
-            tta.at[w, rows_of(i, 0)], ttb.at[w, rows_of(i, 0)], t_send.at[w, i], t_recv.at[w, i], partner
+            tta.at[w, rows_of(j, 0)], ttb.at[w, rows_of(j, 0)], t_send.at[w, j], t_recv.at[w, j], partner
         )
 
-    def f_copy(w, i):
+    def f_copy(w, j):
+        if j in DIRECT:
+            return remote(
+                tta.at[w, rows_of(j, 0)], ttb.at[w, rows_of(j, 96)], f_send.at[w, j], f_recv.at[w, j], across
+            )
         return remote(
-            ttb.at[w, rows_of(i, 0)], ttb.at[w, rows_of(i, 96)], f_send.at[w, i], f_recv.at[w, i], sibling
+            ttb.at[w, rows_of(j, 0)], ttb.at[w, rows_of(j, 96)], f_send.at[w, j], f_recv.at[w, j], sibling
         )
 
     def s_copy(w):
         return remote(tta.at[w, pl.ds(0, 96)], tta.at[w, pl.ds(96, 96)], s_send.at[w], s_recv.at[w], sibling)
 
-    def z_copies(w):
+    def z_copies(w, up):
+        rows = pl.ds(up * 32, 32)
         return [
-            remote(zz.at[w, 1], zz.at[w, 2], z_send.at[w, 0], z_recv.at[w, 0], to_left),
-            remote(zz.at[w, 1], zz.at[w, 0], z_send.at[w, 1], z_recv.at[w, 1], to_right),
+            remote(zz.at[w, 1, rows], zz.at[w, 2, rows], z_send.at[w, up, 0], z_recv.at[w, up, 0], to_left),
+            remote(zz.at[w, 1, rows], zz.at[w, 0, rows], z_send.at[w, up, 1], z_recv.at[w, up, 1], to_right),
         ]
 
     conv_row = lax.broadcasted_iota(jnp.int32, (32, 128), 0) // 2
@@ -102,11 +115,6 @@
     for c in range(16):
         table = jnp.where(conv_row == c, site_ref[c] * 128 + bus_ref[c], table)
     tabs[1] = table
-    parity = lax.rem(lax.broadcasted_iota(jnp.int32, (32, 128), 0), 2)
-    lane = lax.broadcasted_iota(jnp.int32, (32, 128), 1)
-    for g in range(3):
-        hit = (table + parity * 64) == (lane + (me - 1 + g) * 128)
-        ehot[:, g * 128 : g * 128 + 128] = jnp.where(hit, 1.0, 0.0).astype(BF16)
 
     loads[0].wait()
     loads[1].wait()
@@ -120,11 +128,8 @@
 
     lax.fori_loop(0, 16, first, 0, unroll=4)
 
-    pl.semaphore_wait(barrier, 4)
-    for j in range(len(V_RUNS)):
-        for copy in v_copies(0, j):
-            copy.start()
-    for copy in tab_copies:
+    pl.semaphore_wait(barrier, 5)
+    for copy in tab_copies + v_copies(0, 0):
         copy.start()
 
     sub = lax.broadcasted_iota(jnp.int32, (8, 128), 0) // 2
@@ -146,6 +151,41 @@
             return jnp.where(k == 0, at[0], jnp.where(k == 1, at[1], at[2]))
 
         links.append((k0, jnp.clip(pick(k0) - 3, 0, 2), k1, jnp.clip(pick(k1), 0, 8), k2, jnp.clip(pick(k2), 0, 8)))
+
+    def pick_half(w, j):
+        for part in range(3):
+            held = vb[w, j * 8 : j * 8 + 8].reshape(768, 128)[part * 256 : part * 256 + 256]
+            got = lax.dot_general(
+                ehot[...], held, (((1,), (1,)), ((), ())), preferred_element_type=F32
+            ).astype(BF16)
+            at = j * 768 + part * 256
+            for g in range(3):
+                xs[w, g, :, at : at + 256] = got[g * 32 : g * 32 + 32]
+        for copy in x_copies(w, j):
+            copy.start()
+
+    for copy in tab_copies:
+        copy.wait()
+    parity = lax.rem(lax.broadcasted_iota(jnp.int32, (32, 128), 0), 2)
+    lane = lax.broadcasted_iota(jnp.int32, (32, 128), 1)
+    for g in range(3):
+        hit = (tabs[g] + parity * 64) == (lane + me * 128)
+        ehot[g * 32 : g * 32 + 32] = jnp.where(hit, 1.0, 0.0).astype(BF16)
+    for j in range(2):
+        pick_half(0, j)
+
+    row256 = lax.rem(lax.broadcasted_iota(jnp.int32, (16, 256), 0), 2)
+    lane256 = lax.broadcasted_iota(jnp.int32, (16, 256), 1)
+    bus256 = lax.rem(lane256, 64) + me * 128
+    part256 = lane256 // 64
+    for g in range(3):
+        for up in range(2):
+            tab = tabs[g, up * 16 : up * 16 + 16]
+            wide = jnp.concatenate([tab, tab], axis=1)
+            for m in range(2):
+                hit = (wide == bus256) & (part256 == row256 * 2 + m)
+                at = g * 64 + up * 32 + m * 16
+                hh[at : at + 16] = jnp.where(hit, 1.0, 0.0).astype(BF16)
 
     col = lax.broadcasted_iota(jnp.int32, (8, 512), 1)
     slot_bits = jnp.where(col < 256, jnp.where(col >= 96, 1, 0), jnp.where(col >= 384, 3, 2))
@@ -177,44 +217,75 @@
 
         lax.fori_loop(0, 16, own_links, 0, unroll=4)
 
-        sent = 0
-        for j, (start, stop) in enumerate(V_RUNS):
-            for copy in v_copies(w, j):
+        for j in range(2):
+            for copy in x_copies(w, j):
                 copy.wait_recv()
-            count = (stop - start) * 96
-            held = jnp.concatenate(
-                [win[w][g, start:stop].reshape(count, 128) for g in range(3)], axis=1
-            )
-            xs[:, start * 96 : stop * 96] = lax.dot_general(
-                ehot[...], held, (((1,), (1,)), ((), ())), preferred_element_type=F32
-            )
-            while sent < len(T_RUNS) and T_AFTER[sent] == j:
-                for tp in range(T_RUNS[sent][0] // 16, T_RUNS[sent][1] // 16):
-                    for u in range(4):
-                        swapped = [
-                            block_swap(xs[u * 8 : u * 8 + 8, t * 128 : t * 128 + 128], masks)
-                            for t in (2 * tp, 2 * tp + 1)
-                        ]
+            for tp in range(3 * j, 3 * j + 3):
+                for up in range(2):
+                    both = []
+                    for t in (2 * tp, 2 * tp + 1):
+                        rows, lanes = slice(up * 16, up * 16 + 16), slice(t * 128, t * 128 + 128)
+                        both.append(
+                            xs[w, 1, rows, lanes].astype(F32)
+                            + xr[w, 0, rows, lanes].astype(F32)
+                            + xr[w, 1, rows, lanes].astype(F32)
+                        )
+                    for half in range(2):
+                        u = up * 2 + half
+                        swapped = [block_swap(b[half * 8 : half * 8 + 8], masks) for b in both]
                         tta[w, tp * 16 : tp * 16 + 16, u * 128 : u * 128 + 128] = jnp.concatenate(
                             swapped, axis=0
                         ).astype(BF16)
-                t_copy(w, sent).start()
-                sent += 1
+            t_copy(w, j).start()
+            if j in DIRECT:
+                f_copy(w, j).start()
         s_copy(w).start()
 
-        if w == 0:
-            for copy in tab_copies:
-                copy.wait()
-            row256 = lax.rem(lax.broadcasted_iota(jnp.int32, (32, 256), 0), 2)
-            lane256 = lax.broadcasted_iota(jnp.int32, (32, 256), 1)
-            bus256 = lax.rem(lane256, 64) + me * 128
-            part256 = lane256 // 64
-            for g in range(3):
-                wide = jnp.concatenate([tabs[g], tabs[g]], axis=1)
-                for m in range(2):
-                    hit = (wide == bus256) & (part256 == row256 * 2 + m)
-                    at = g * 64 + m * 32
-                    hh[at : at + 32] = jnp.where(hit, 1.0, 0.0).astype(BF16)
+        def couple(held, top, rows, at, add, tiles=range(4)):
+            for u in tiles:
+                rhs = held[w, top : top + rows, u * 128 : u * 128 + 128]
+                total = None
+                for q in range(4):
+                    c = u * 4 + q
+                    one = dot(bp[c * 96 : c * 96 + 96, at : at + rows], rhs)
+                    total = one if total is None else jnp.where(chunk_masks[q], one, total)
+                lanes = slice(u * 128, u * 128 + 128)
+                cur[:, lanes] = cur[:, lanes] + total if add else total
+
+        for j in range(2):
+            t_copy(w, j).wait_send()
+            if j in DIRECT:
+                f_copy(w, j).wait_send()
+        for copy in v_copies(w, 1):
+            copy.start()
+        s_copy(w).wait_recv()
+        couple(tta, 0, 192, 0, False)
+        for j in range(2):
+            t_copy(w, j).wait_recv()
+            if j not in DIRECT:
+                f_copy(w, j).start()
+        couple(ttb, 0, 96, 256, True)
+        for j in range(2):
+            f_copy(w, j).wait_recv()
+
+        for up in range(2):
+            couple(ttb, 96, 96, 384, True, (2 * up, 2 * up + 1))
+            for j in range(12):
+                m, ph = j // 6, j % 6
+                swapped = [
+                    block_swap(cur[j * 8 : j * 8 + 8, u * 128 : u * 128 + 128], masks)
+                    for u in (2 * up, 2 * up + 1)
+                ]
+                at = up * 32 + m * 16
+                zz[w, 1, at : at + 16, ph * 128 : ph * 128 + 128] = jnp.concatenate(
+                    swapped, axis=0
+                ).astype(BF16)
+            for copy in z_copies(w, up):
+                copy.start()
+
+        for j in range(2):
+            for copy in v_copies(w, j):
+                copy.wait_recv()
 
         def other_links(h, carry):
             for p in range(3):
@@ -228,42 +299,9 @@
 
         lax.fori_loop(0, 16, other_links, 0, unroll=4)
 
-        def couple(held, top, rows, at, add):
-            for u in range(4):
-                rhs = held[w, top : top + rows, u * 128 : u * 128 + 128]
-                total = None
-                for q in range(4):
-                    c = u * 4 + q
-                    one = dot(bp[c * 96 : c * 96 + 96, at : at + rows], rhs)
-                    total = one if total is None else jnp.where(chunk_masks[q], one, total)
-                lanes = slice(u * 128, u * 128 + 128)
-                cur[:, lanes] = cur[:, lanes] + total if add else total
-
-        s_copy(w).wait_recv()
-        couple(tta, 0, 192, 0, False)
-        for i in range(len(T_RUNS)):
-            t_copy(w, i).wait_recv()
-            f_copy(w, i).start()
-        couple(ttb, 0, 96, 256, True)
-        for i in range(len(T_RUNS)):
-            f_copy(w, i).wait_recv()
-        couple(ttb, 96, 96, 384, True)
-
         for up in range(2):
-            for j in range(12):
-                m, ph = j // 6, j % 6
-                swapped = [
-                    block_swap(cur[j * 8 : j * 8 + 8, u * 128 : u * 128 + 128], masks)
-                    for u in (2 * up, 2 * up + 1)
-                ]
-                at = m * 32 + up * 16
-                zz[w, 1, at : at + 16, ph * 128 : ph * 128 + 128] = jnp.concatenate(
-                    swapped, axis=0
-                ).astype(BF16)
-        for copy in z_copies(w):
-            copy.start()
-        for copy in z_copies(w):
-            copy.wait_recv()
+            for copy in z_copies(w, up):
+                copy.wait_recv()
         spread[...] = lax.dot_general(
             zz[w].reshape(192, 768), hh[...], (((0,), (0,)), ((), ())), preferred_element_type=F32
         )
@@ -283,25 +321,23 @@
             return carry
 
         if w < ITERS - 1:
-            for j, (start, stop) in enumerate(V_RUNS):
-                lax.fori_loop(start, stop, finish, 0, unroll=stop - start)
-                for copy in v_copies(w + 1, j):
-                    copy.start()
+            for j in range(2):
+                lax.fori_loop(j * 8, j * 8 + 8, finish, 0, unroll=4)
+                pick_half(w + 1, j)
+            for copy in v_copies(w + 1, 0):
+                copy.start()
         else:
             lax.fori_loop(0, 16, finish, 0, unroll=4)
 
     result = pltpu.make_async_copy(resid, out_hbm, out_sem)
     result.start()
     for w in range(ITERS):
-        for j in range(len(V_RUNS)):
-            for copy in v_copies(w, j):
+        for j in range(2):
+            for copy in v_copies(w, j) + x_copies(w, j) + z_copies(w, j):
                 copy.wait_send()
-        for i in range(len(T_RUNS)):
-            t_copy(w, i).wait_send()
-            f_copy(w, i).wait_send()
+            if j not in DIRECT:
+                f_copy(w, j).wait_send()
         s_copy(w).wait_send()
-        for copy in z_copies(w):
-            copy.wait_send()
     result.wait()
 
 
@@ -321,7 +357,6 @@
     vmem = pl.BlockSpec(memory_space=pltpu.VMEM)
     dma = pltpu.SemaphoreType.DMA
     tiles = (16, 3, 32, 128)
-    runs, parts = len(V_RUNS), len(T_RUNS)
     residual = pl.pallas_call(
         functools.partial(kernel, n_bus),
         out_shape=jax.ShapeDtypeStruct(tiles, BF16),
@@ -338,10 +373,11 @@
             pltpu.VMEM((3,) + tiles, BF16),
             pltpu.VMEM((3,) + tiles, BF16),
             pltpu.VMEM((3, 32, 128), jnp.int32),
-            pltpu.VMEM((32, 384), BF16),
+            pltpu.VMEM((96, 128), BF16),
             pltpu.VMEM((192, 256), BF16),
             pltpu.VMEM(tiles, F32),
-            pltpu.VMEM((32, 1536), F32),
+            pltpu.VMEM((ITERS, 3, 32, 1536), BF16),
+            pltpu.VMEM((ITERS, 2, 32, 1536), BF16),
             pltpu.VMEM((ITERS, 192, 512), BF16),
             pltpu.VMEM((ITERS, 192, 512), BF16),
             pltpu.VMEM((96, 512), F32),
@@ -349,16 +385,18 @@
             pltpu.VMEM((768, 256), F32),
             pltpu.VMEM(tiles, BF16),
             dma((4,)),
-            dma((ITERS, runs, 2)),
-            dma((ITERS, runs, 2)),
-            dma((ITERS, parts)),
-            dma((ITERS, parts)),
-            dma((ITERS, parts)),
-            dma((ITERS, parts)),
+            dma((ITERS, 2, 2)),
+            dma((ITERS, 2, 2)),
+            dma((ITERS, 2, 2)),
+            dma((ITERS, 2, 2)),
+            dma((ITERS, 2)),
+            dma((ITERS, 2)),
+            dma((ITERS, 2)),
+            dma((ITERS, 2)),
             dma((ITERS,)),
             dma((ITERS,)),
-            dma((ITERS, 2)),
-            dma((ITERS, 2)),
+            dma((ITERS, 2, 2)),
+            dma((ITERS, 2, 2)),
             dma((2,)),
             dma((2,)),
             dma,

time: 69.5 us -> 66.3 us (0.954)
  Pallas kernels: 67 us -> 63.7 us
    pallas_call x1, Pallas kernels: 67 us -> 63.7 us  [per_device(): pl.pallas_call(functools.partial(kernel, n_bus), out_shape=jax.ShapeDtype...]
where the time goes in v3:
time: 66.3 us; the launch traced here: 66.1 us
  Pallas kernels  63.7 us (96%)
  matrix products  2.4 us (4%)
    pallas_call x1, Pallas kernels, per_device(): pl.pallas_call(functools.partial(kernel, n_bus), out_shape=jax.ShapeDtype...  63.7 us
    dot_general x1, matrix products, per_device(): jnp.einsum('htsa,htab->htsb', residual, inv_diag, preferred_element_type=...  2.4 us

profile of v3, /device:TPU:1, one launch (start us, length us, event | category | flops | bytes accessed | tf_op | source)
XLA Modules:
  0.0 66.1 jit_solution(8414203591825853714)
XLA Ops:
  0.0 0.0 copy-start
  0.0 63.7 %shard_map.82 = bf16[16,3,32,128]{3,2,1,0:T(8,128)(2,1)} custom-call(s32[16]{0:T(128)} %site_ref.1, s32[16]{0:T(128)} %bus_ref.1, s32[3,3]{1,0:T(4,128)} %pat_ref.1, s32[8,512]{1,0:T(8,128)} %constant.2.clone.order_ref, bf16[16,3,32,128]{3,2,1,0:T(8,128)(2,1)} %inj_hbm.1, bf16[16,3,128,128]{3,2,1,0:T(8,128)(2,1)} %inv_hbm.1, ...), custom_call_target="tpu_custom_call" | custom-call | tf_op jit(solution)/shard_map/pallas_call | solution.py:360
  63.7 0.0 copy-done
  63.7 2.4 %fusion = f32[16,3,32,128]{3,2,1,0:T(8,128)} fusion(bf16[16,3,32,128]{3,2,1,0:T(8,128)(2,1)} %shard_map.82, bf16[16,3,128,128]{3,2,1,0:T(8,128)(2,1)S(1)} %copy-done), kind=kOutput, calls=%fused_computation | convolution fusion | flops 50331648 | bytes 2752512 | tf_op jit(solution)/shard_map/htsa,htab->htsb/dot_general | solution.py:417
Async XLA Ops:
  0.0 63.7 %copy-start = (bf16[16,3,128,128]{3,2,1,0:T(8,128)(2,1)S(1)}, bf16[16,3,128,128]{3,2,1,0:T(8,128)(2,1)}, u32[]{:S(2)}) copy-start(bf16[16,3,128,128]{3,2,1,0:T(8,128)(2,1)} %inv_hbm.1) | copy-start | bytes 4718596

commit v4 on v3

--- a/solution.py
+++ b/solution.py
@@ -15,7 +15,6 @@
 
 V_RUNS = ((0, 8), (8, 16))
 HALF_ROWS = 48
-DIRECT = ()
 
 
 def dot(a, b):
@@ -34,7 +33,7 @@
     n_bus,
     site_ref, bus_ref, pat_ref, order_ref, inj_hbm, inv_hbm, off_hbm, cpl_hbm,
     out_hbm,
-    inj, inv, off, cpl, perm, bp, vb, win_0, win_1, tabs, ehot, hh, base, xs, xr, tta, ttb, cur, zz, spread, resid,
+    inj, inv, off, cpl, perm, bp, vb, win_0, win_1, tabs, ehot, wide_hot, hh, base, picked, xs, xr, tta, ttb, cur, zz, spread, resid,
     load_sem, v_send, v_recv, x_send, x_recv, t_send, t_recv, f_send, f_recv, s_send, s_recv, z_send, z_recv, tab_send, tab_recv, out_sem,
 ):
     win = (win_0, win_1)
@@ -46,7 +45,6 @@
     to_left, to_right = (left, harm), (right, harm)
     sibling = (me, zh * 2 + 1 - core)
     partner = (me, (1 - zh) * 2 + core)
-    across = (me, (1 - zh) * 2 + 1 - core)
 
     loads = [
         pltpu.make_async_copy(src, dst, load_sem.at[i])
@@ -56,7 +54,7 @@
         load.start()
 
     barrier = pltpu.get_barrier_semaphore()
-    for peer in (to_left, to_right, sibling, partner, across):
+    for peer in (to_left, to_right, sibling, partner):
         pl.semaphore_signal(barrier, inc=1, device_id=peer, device_id_type=MESH)
 
     def remote(src, dst, send, recv, peer):
@@ -92,10 +90,6 @@
         )
 
     def f_copy(w, j):
-        if j in DIRECT:
-            return remote(
-                tta.at[w, rows_of(j, 0)], ttb.at[w, rows_of(j, 96)], f_send.at[w, j], f_recv.at[w, j], across
-            )
         return remote(
             ttb.at[w, rows_of(j, 0)], ttb.at[w, rows_of(j, 96)], f_send.at[w, j], f_recv.at[w, j], sibling
         )
@@ -115,6 +109,11 @@
     for c in range(16):
         table = jnp.where(conv_row == c, site_ref[c] * 128 + bus_ref[c], table)
     tabs[1] = table
+    parity = lax.rem(lax.broadcasted_iota(jnp.int32, (32, 128), 0), 2)
+    lane = lax.broadcasted_iota(jnp.int32, (32, 128), 1)
+    for g in range(3):
+        hit = (table + parity * 64) == (lane + (me - 1 + g) * 128)
+        wide_hot[:, g * 128 : g * 128 + 128] = jnp.where(hit, 1.0, 0.0).astype(BF16)
 
     loads[0].wait()
     loads[1].wait()
@@ -128,7 +127,7 @@
 
     lax.fori_loop(0, 16, first, 0, unroll=4)
 
-    pl.semaphore_wait(barrier, 5)
+    pl.semaphore_wait(barrier, 4)
     for copy in tab_copies + v_copies(0, 0):
         copy.start()
 
@@ -166,13 +165,10 @@
 
     for copy in tab_copies:
         copy.wait()
-    parity = lax.rem(lax.broadcasted_iota(jnp.int32, (32, 128), 0), 2)
-    lane = lax.broadcasted_iota(jnp.int32, (32, 128), 1)
     for g in range(3):
         hit = (tabs[g] + parity * 64) == (lane + me * 128)
         ehot[g * 32 : g * 32 + 32] = jnp.where(hit, 1.0, 0.0).astype(BF16)
-    for j in range(2):
-        pick_half(0, j)
+    pick_half(0, 1)
 
     row256 = lax.rem(lax.broadcasted_iota(jnp.int32, (16, 256), 0), 2)
     lane256 = lax.broadcasted_iota(jnp.int32, (16, 256), 1)
@@ -207,6 +203,11 @@
     lax.fori_loop(0, 16, permute, 0)
     loads[3].wait()
 
+    results = []
+    for j in range(2):
+        half = pl.ds(j * 8, 8)
+        results.append(pltpu.make_async_copy(resid.at[half], out_hbm.at[half], out_sem.at[j]))
+
     for w in range(ITERS):
 
         def own_links(h, carry):
@@ -218,13 +219,31 @@
         lax.fori_loop(0, 16, own_links, 0, unroll=4)
 
         for j in range(2):
-            for copy in x_copies(w, j):
-                copy.wait_recv()
+            if (w, j) == (0, 0):
+                for copy in v_copies(0, 0):
+                    copy.wait_recv()
+                for part in range(3):
+                    held = jnp.concatenate(
+                        [
+                            win[0][g, 0:8].reshape(768, 128)[part * 256 : part * 256 + 256]
+                            for g in range(3)
+                        ],
+                        axis=1,
+                    )
+                    picked[:, part * 256 : part * 256 + 256] = lax.dot_general(
+                        wide_hot[...], held, (((1,), (1,)), ((), ())), preferred_element_type=F32
+                    )
+            else:
+                for copy in x_copies(w, j):
+                    copy.wait_recv()
             for tp in range(3 * j, 3 * j + 3):
                 for up in range(2):
                     both = []
                     for t in (2 * tp, 2 * tp + 1):
                         rows, lanes = slice(up * 16, up * 16 + 16), slice(t * 128, t * 128 + 128)
+                        if (w, j) == (0, 0):
+                            both.append(picked[rows, lanes])
+                            continue
                         both.append(
                             xs[w, 1, rows, lanes].astype(F32)
                             + xr[w, 0, rows, lanes].astype(F32)
@@ -237,8 +256,6 @@
                             swapped, axis=0
                         ).astype(BF16)
             t_copy(w, j).start()
-            if j in DIRECT:
-                f_copy(w, j).start()
         s_copy(w).start()
 
         def couple(held, top, rows, at, add, tiles=range(4)):
@@ -254,16 +271,13 @@
 
         for j in range(2):
             t_copy(w, j).wait_send()
-            if j in DIRECT:
-                f_copy(w, j).wait_send()
         for copy in v_copies(w, 1):
             copy.start()
         s_copy(w).wait_recv()
         couple(tta, 0, 192, 0, False)
         for j in range(2):
             t_copy(w, j).wait_recv()
-            if j not in DIRECT:
-                f_copy(w, j).start()
+            f_copy(w, j).start()
         couple(ttb, 0, 96, 256, True)
         for j in range(2):
             f_copy(w, j).wait_recv()
@@ -280,12 +294,14 @@
                 zz[w, 1, at : at + 16, ph * 128 : ph * 128 + 128] = jnp.concatenate(
                     swapped, axis=0
                 ).astype(BF16)
+        for up in range(2):
             for copy in z_copies(w, up):
                 copy.start()
 
         for j in range(2):
-            for copy in v_copies(w, j):
-                copy.wait_recv()
+            if (w, j) != (0, 0):
+                for copy in v_copies(w, j):
+                    copy.wait_recv()
 
         def other_links(h, carry):
             for p in range(3):
@@ -302,9 +318,16 @@
         for up in range(2):
             for copy in z_copies(w, up):
                 copy.wait_recv()
-        spread[...] = lax.dot_general(
-            zz[w].reshape(192, 768), hh[...], (((0,), (0,)), ((), ())), preferred_element_type=F32
-        )
+
+        def spread_half(j):
+            for p in range(3):
+                at = p * 256 + j * 128
+                spread[at : at + 128] = lax.dot_general(
+                    zz[w, :, :, at : at + 128].reshape(192, 128),
+                    hh[...],
+                    (((0,), (0,)), ((), ())),
+                    preferred_element_type=F32,
+                )
 
         def finish(h, carry):
             hq, e = h // 2, lax.rem(h, 2)
@@ -322,23 +345,26 @@
 
         if w < ITERS - 1:
             for j in range(2):
-                lax.fori_loop(j * 8, j * 8 + 8, finish, 0, unroll=4)
+                spread_half(j)
+                lax.fori_loop(j * 8, j * 8 + 8, finish, 0, unroll=8)
                 pick_half(w + 1, j)
             for copy in v_copies(w + 1, 0):
                 copy.start()
         else:
-            lax.fori_loop(0, 16, finish, 0, unroll=4)
-
-    result = pltpu.make_async_copy(resid, out_hbm, out_sem)
-    result.start()
+            for j in range(2):
+                spread_half(j)
+                lax.fori_loop(j * 8, j * 8 + 8, finish, 0, unroll=4)
+                results[j].start()
+
     for w in range(ITERS):
         for j in range(2):
-            for copy in v_copies(w, j) + x_copies(w, j) + z_copies(w, j):
+            picks = [] if (w, j) == (0, 0) else x_copies(w, j)
+            for copy in v_copies(w, j) + picks + z_copies(w, j):
                 copy.wait_send()
-            if j not in DIRECT:
-                f_copy(w, j).wait_send()
+            f_copy(w, j).wait_send()
         s_copy(w).wait_send()
-    result.wait()
+    for copy in results:
+        copy.wait()
 
 
 def column_order():
@@ -374,8 +400,10 @@
             pltpu.VMEM((3,) + tiles, BF16),
             pltpu.VMEM((3, 32, 128), jnp.int32),
             pltpu.VMEM((96, 128), BF16),
+            pltpu.VMEM((32, 384), BF16),
             pltpu.VMEM((192, 256), BF16),
             pltpu.VMEM(tiles, F32),
+            pltpu.VMEM((32, 768), F32),
             pltpu.VMEM((ITERS, 3, 32, 1536), BF16),
             pltpu.VMEM((ITERS, 2, 32, 1536), BF16),
             pltpu.VMEM((ITERS, 192, 512), BF16),
@@ -399,7 +427,7 @@
             dma((ITERS, 2, 2)),
             dma((2,)),
             dma((2,)),
-            dma,
+            dma((2,)),
         ],
         compiler_params=pltpu.CompilerParams(
             collective_id=0, has_side_effects=True, vmem_limit_bytes=56 << 20
@@ -414,7 +442,10 @@
         off_tiles,
         coupling.reshape(1536, 384),
     )
-    return jnp.einsum("htsa,htab->htsb", residual, inv_diag, preferred_element_type=F32)
+    last = jnp.einsum(
+        "tsa,tab->tsb", residual.reshape(48, 32, 128), inv_diag.reshape(48, 128, 128), preferred_element_type=F32
+    )
+    return last.reshape(tiles)
 
 
 def solution(mesh):

time: 66.3 us -> 65.4 us (0.986)
  Pallas kernels: 63.7 us -> 62.9 us
    pallas_call x1, Pallas kernels: 63.7 us -> 62.9 us  [per_device(): pl.pallas_call(functools.partial(kernel, n_bus), out_shape=jax.ShapeDtype...]
where the time goes in v4:
time: 65.4 us; the launch traced here: 65.3 us
  Pallas kernels  62.9 us (96%)
  matrix products  2.4 us (4%)
    pallas_call x1, Pallas kernels, per_device(): pl.pallas_call(functools.partial(kernel, n_bus), out_shape=jax.ShapeDtype...  62.9 us
    dot_general x1, matrix products, per_device(): jnp.einsum('tsa,tab->tsb', residual.reshape(48, 32, 128), inv_diag.reshap...  2.4 us

profile of v4, /device:TPU:1, one launch (start us, length us, event | category | flops | bytes accessed | tf_op | source)
XLA Modules:
  0.0 65.3 jit_solution(17743397097269004439)
XLA Ops:
  0.0 0.0 copy-start
  0.0 62.9 %shard_map.82 = bf16[16,3,32,128]{3,2,1,0:T(8,128)(2,1)} custom-call(s32[16]{0:T(128)} %site_ref.1, s32[16]{0:T(128)} %bus_ref.1, s32[3,3]{1,0:T(4,128)} %pat_ref.1, s32[8,512]{1,0:T(8,128)} %constant.2.clone.order_ref, bf16[16,3,32,128]{3,2,1,0:T(8,128)(2,1)} %inj_hbm.1, bf16[16,3,128,128]{3,2,1,0:T(8,128)(2,1)} %inv_hbm.1, ...), custom_call_target="tpu_custom_call" | custom-call | tf_op jit(solution)/shard_map/pallas_call | solution.py:386
  62.9 0.0 copy-done
  62.9 2.4 %fusion = f32[48,32,128]{2,1,0:T(8,128)} fusion(bf16[48,32,128]{2,1,0:T(8,128)(2,1)} %bitcast.7, bf16[48,128,128]{2,1,0:T(8,128)(2,1)S(1)} %bitcast.6), kind=kOutput, calls=%fused_computation | convolution fusion | flops 50331648 | bytes 2752512 | tf_op jit(solution)/shard_map/tsa,tab->tsb/dot_general | solution.py:445
Async XLA Ops:
  0.0 62.9 %copy-start = (bf16[16,3,128,128]{3,2,1,0:T(8,128)(2,1)S(1)}, bf16[16,3,128,128]{3,2,1,0:T(8,128)(2,1)}, u32[]{:S(2)}) copy-start(bf16[16,3,128,128]{3,2,1,0:T(8,128)(2,1)} %inv_hbm.1) | copy-start | bytes 4718596

commit v5 on v4

--- a/solution.py
+++ b/solution.py
@@ -13,7 +13,7 @@
 F32 = jnp.float32
 BF16 = jnp.bfloat16
 
-V_RUNS = ((0, 8), (8, 16))
+V_RUNS = (((0, 8), (8, 16)), ((0, 6), (6, 16)))
 HALF_ROWS = 48
 
 
@@ -68,7 +68,7 @@
     ]
 
     def v_copies(w, j):
-        run = pl.ds(V_RUNS[j][0], V_RUNS[j][1] - V_RUNS[j][0])
+        run = pl.ds(V_RUNS[w][j][0], V_RUNS[w][j][1] - V_RUNS[w][j][0])
         return [
             remote(vb.at[w, run], win[w].at[2, run], v_send.at[w, j, 0], v_recv.at[w, j, 0], to_left),
             remote(vb.at[w, run], win[w].at[0, run], v_send.at[w, j, 1], v_recv.at[w, j, 1], to_right),
@@ -97,11 +97,10 @@
     def s_copy(w):
         return remote(tta.at[w, pl.ds(0, 96)], tta.at[w, pl.ds(96, 96)], s_send.at[w], s_recv.at[w], sibling)
 
-    def z_copies(w, up):
-        rows = pl.ds(up * 32, 32)
+    def z_copies(w):
         return [
-            remote(zz.at[w, 1, rows], zz.at[w, 2, rows], z_send.at[w, up, 0], z_recv.at[w, up, 0], to_left),
-            remote(zz.at[w, 1, rows], zz.at[w, 0, rows], z_send.at[w, up, 1], z_recv.at[w, up, 1], to_right),
+            remote(zz.at[w, 1], zz.at[w, 2], z_send.at[w, 0], z_recv.at[w, 0], to_left),
+            remote(zz.at[w, 1], zz.at[w, 0], z_send.at[w, 1], z_recv.at[w, 1], to_right),
         ]
 
     conv_row = lax.broadcasted_iota(jnp.int32, (32, 128), 0) // 2
@@ -294,9 +293,8 @@
                 zz[w, 1, at : at + 16, ph * 128 : ph * 128 + 128] = jnp.concatenate(
                     swapped, axis=0
                 ).astype(BF16)
-        for up in range(2):
-            for copy in z_copies(w, up):
-                copy.start()
+        for copy in z_copies(w):
+            copy.start()
 
         for j in range(2):
             if (w, j) != (0, 0):
@@ -315,9 +313,8 @@
 
         lax.fori_loop(0, 16, other_links, 0, unroll=4)
 
-        for up in range(2):
-            for copy in z_copies(w, up):
-                copy.wait_recv()
+        for copy in z_copies(w):
+            copy.wait_recv()
 
         def spread_half(j):
             for p in range(3):
@@ -359,10 +356,11 @@
     for w in range(ITERS):
         for j in range(2):
             picks = [] if (w, j) == (0, 0) else x_copies(w, j)
-            for copy in v_copies(w, j) + picks + z_copies(w, j):
+            for copy in v_copies(w, j) + picks:
                 copy.wait_send()
             f_copy(w, j).wait_send()
-        s_copy(w).wait_send()
+        for copy in z_copies(w) + [s_copy(w)]:
+            copy.wait_send()
     for copy in results:
         copy.wait()
 
@@ -423,8 +421,8 @@
             dma((ITERS, 2)),
             dma((ITERS,)),
             dma((ITERS,)),
-            dma((ITERS, 2, 2)),
-            dma((ITERS, 2, 2)),
+            dma((ITERS, 2)),
+            dma((ITERS, 2)),
             dma((2,)),
             dma((2,)),
             dma((2,)),

time: 65.4 us -> 65.6 us (level)
  no operation moved by 1% of the time
where the time goes in v5:
time: 65.6 us; the launch traced here: 65.5 us
  Pallas kernels  63.1 us (96%)
  matrix products  2.4 us (4%)
    pallas_call x1, Pallas kernels, per_device(): pl.pallas_call(functools.partial(kernel, n_bus), out_shape=jax.ShapeDtype...  63.1 us
    dot_general x1, matrix products, per_device(): jnp.einsum('tsa,tab->tsb', residual.reshape(48, 32, 128), inv_diag.reshap...  2.4 us

profile of v5, /device:TPU:1, one launch (start us, length us, event | category | flops | bytes accessed | tf_op | source)
XLA Modules:
  0.0 65.5 jit_solution(7508482257797935704)
XLA Ops:
  0.0 0.0 copy-start
  0.0 63.1 %shard_map.82 = bf16[16,3,32,128]{3,2,1,0:T(8,128)(2,1)} custom-call(s32[16]{0:T(128)} %site_ref.1, s32[16]{0:T(128)} %bus_ref.1, s32[3,3]{1,0:T(4,128)} %pat_ref.1, s32[8,512]{1,0:T(8,128)} %constant.2.clone.order_ref, bf16[16,3,32,128]{3,2,1,0:T(8,128)(2,1)} %inj_hbm.1, bf16[16,3,128,128]{3,2,1,0:T(8,128)(2,1)} %inv_hbm.1, ...), custom_call_target="tpu_custom_call" | custom-call | tf_op jit(solution)/shard_map/pallas_call | solution.py:384
  63.1 0.0 copy-done
  63.1 2.4 %fusion = f32[48,32,128]{2,1,0:T(8,128)} fusion(bf16[48,32,128]{2,1,0:T(8,128)(2,1)} %bitcast.7, bf16[48,128,128]{2,1,0:T(8,128)(2,1)S(1)} %bitcast.6), kind=kOutput, calls=%fused_computation | convolution fusion | flops 50331648 | bytes 2752512 | tf_op jit(solution)/shard_map/tsa,tab->tsb/dot_general | solution.py:443
Async XLA Ops:
  0.0 63.1 %copy-start = (bf16[16,3,128,128]{3,2,1,0:T(8,128)(2,1)S(1)}, bf16[16,3,128,128]{3,2,1,0:T(8,128)(2,1)}, u32[]{:S(2)}) copy-start(bf16[16,3,128,128]{3,2,1,0:T(8,128)(2,1)} %inv_hbm.1) | copy-start | bytes 4718596

commit v6 on v5

--- a/solution.py
+++ b/solution.py
@@ -350,7 +350,7 @@
         else:
             for j in range(2):
                 spread_half(j)
-                lax.fori_loop(j * 8, j * 8 + 8, finish, 0, unroll=4)
+                lax.fori_loop(j * 8, j * 8 + 8, finish, 0, unroll=8)
                 results[j].start()
 
     for w in range(ITERS):

time: 65.6 us -> 65.2 us (level)
  no operation moved by 1% of the time
where the time goes in v6:
time: 65.2 us
  Pallas kernels  62.8 us (96%)
  matrix products  2.4 us (4%)
    pallas_call x1, Pallas kernels, per_device(): pl.pallas_call(functools.partial(kernel, n_bus), out_shape=jax.ShapeDtype...  62.8 us
    dot_general x1, matrix products, per_device(): jnp.einsum('tsa,tab->tsb', residual.reshape(48, 32, 128), inv_diag.reshap...  2.4 us

profile of v6, /device:TPU:1, one launch (start us, length us, event | category | flops | bytes accessed | tf_op | source)
XLA Modules:
  0.0 65.2 jit_solution(11575634381864040761)
XLA Ops:
  0.0 0.0 copy-start
  0.0 62.8 %shard_map.82 = bf16[16,3,32,128]{3,2,1,0:T(8,128)(2,1)} custom-call(s32[16]{0:T(128)} %site_ref.1, s32[16]{0:T(128)} %bus_ref.1, s32[3,3]{1,0:T(4,128)} %pat_ref.1, s32[8,512]{1,0:T(8,128)} %constant.2.clone.order_ref, bf16[16,3,32,128]{3,2,1,0:T(8,128)(2,1)} %inj_hbm.1, bf16[16,3,128,128]{3,2,1,0:T(8,128)(2,1)} %inv_hbm.1, ...), custom_call_target="tpu_custom_call" | custom-call | tf_op jit(solution)/shard_map/pallas_call | solution.py:384
  62.8 0.0 copy-done
  62.8 2.4 %fusion = f32[48,32,128]{2,1,0:T(8,128)} fusion(bf16[48,32,128]{2,1,0:T(8,128)(2,1)} %bitcast.7, bf16[48,128,128]{2,1,0:T(8,128)(2,1)S(1)} %bitcast.6), kind=kOutput, calls=%fused_computation | convolution fusion | flops 50331648 | bytes 2752512 | tf_op jit(solution)/shard_map/tsa,tab->tsb/dot_general | solution.py:443
Async XLA Ops:
  0.0 62.8 %copy-start = (bf16[16,3,128,128]{3,2,1,0:T(8,128)(2,1)S(1)}, bf16[16,3,128,128]{3,2,1,0:T(8,128)(2,1)}, u32[]{:S(2)}) copy-start(bf16[16,3,128,128]{3,2,1,0:T(8,128)(2,1)} %inv_hbm.1) | copy-start | bytes 4718596
